TPU v7x, 128 devices: a whole 4x4x4 slice. The times are simulated.
128 devices in a mesh: sec: 4 (over x), blk: 32 (over y, z, core).
Axes of the slice: x: 4, y: 4, z: 4, core: 2. Of those that a mesh axis runs over, the one named last changes fastest.
Arguments:
- state: float32 [2, 72, 16384], P(None, None, ('sec', 'blk')), may hold values from -6 to 6
- neighbors: int32 [4, 16384], P(None, ('sec', 'blk')), may hold values from 0 to 16383, as said below
- owner: int32 [16384, 1], P(('sec', 'blk')), may hold values from 0 to 127; in each aligned block of 128 rows (0 to 127, 128 to 255, ...) at most 2 rows name the same one
- crm_state: bfloat16 [32768, 9216], P(('sec', 'blk')), may hold values from -6 to 6
- phase_mask: int32 [32768, 4608], P(('sec', 'blk')), may hold values 0 or 1
Outputs:
- new_state: float32 [2, 72, 16384], P(None, None, ('sec', 'blk'))
Inputs may be any that keep to these rules, and one draw needn't show every extreme that they name: `neighbors`: each entry is a column index within 8 of its own column's index, counted cyclically over 16384. Among the columns of one device no owner is named more than 2 times.
All inputs are finite; a program needn't handle non-finite values. No bound on the sum of `phase_mask` on one device may be relied on, other than what follows from the above.
Results may differ from a plain program's by a relative error of at most 0.0003.
Values sent between devices are 32-bit elements; how exact they have to be, the bound alone decides.
A program may use at most 128 MiB of HBM per device.

v0:
```python
import jax
import jax.numpy as jnp
from jax import lax
from jax.sharding import PartitionSpec as P

SUB = 4
REACH = 8


def extended(array, sides, width):
    for axis, dim in sides:
        size, length = (lax.axis_size(axis), array.shape[dim])
        up = [(i, (i + 1) % size) for i in range(size)]
        down = [(j, i) for i, j in up]
        last = lax.slice_in_dim(array, length - width, length, axis=dim)
        first = lax.slice_in_dim(array, 0, width, axis=dim)
        before = lax.ppermute(last, axis, up)
        after = lax.ppermute(first, axis, down)
        array = jnp.concatenate([before, array, after], axis=dim)
    return array


def condense(temp_col, moist_col, temp_force, moist_force, pert, flags):
    count = pert.shape[0]
    levels = temp_col.shape[1]
    fields = pert.astype(jnp.float32).reshape(count, 2, levels, -1)
    temper = temp_col[:, :, None] + fields[:, 0]
    moisture = moist_col[:, :, None] + fields[:, 1]
    is_ice = flags.reshape(count, levels, -1) == 1
    rate = jnp.where(is_ice, 0.3, 0.7).astype(jnp.float32)
    heat = jnp.where(is_ice, 1.3, 1.0).astype(jnp.float32)
    for substep in range(SUB):
        temper = temper + 0.2 * (jnp.roll(temper, 1, 2) + jnp.roll(temper, -1, 2) - 2.0 * temper)
        moisture = moisture + 0.2 * (
            jnp.roll(moisture, 1, 2) + jnp.roll(moisture, -1, 2) - 2.0 * moisture
        )
        temper = temper + temp_force[:, :, None] / SUB
        moisture = moisture + moist_force[:, :, None] / SUB
        excess = moisture - 0.8 * jnp.exp(0.3 * temper)
        cond = rate * jnp.maximum(excess, 0.0)
        moisture = moisture - cond
        temper = temper + heat * cond
    return (jnp.mean(temper, axis=2) - temp_col, jnp.mean(moisture, axis=2) - moist_col)


def local(state, neighbors, owner, crm_state, phase_mask):
    ndev = lax.axis_size(("sec", "blk"))
    myself = lax.axis_index(("sec", "blk"))
    levels = state.shape[1]
    cdev = state.shape[2]
    total = cdev * ndev
    slots = crm_state.shape[0]
    cap = slots // ndev
    widened = extended(state, ((("sec", "blk"), 2),), REACH)
    first = myself * cdev - REACH
    local_index = jnp.mod(neighbors - first, total)
    near = jnp.zeros_like(state)
    for k in range(4):
        near = near + jnp.take(widened, local_index[k], axis=2)
    dyn = 0.15 * (near - 4.0 * state)
    payload = jnp.concatenate([state, dyn], axis=0).reshape(4 * levels, cdev)
    mine = owner[:, 0]
    order = jnp.arange(cdev, dtype=jnp.int32)
    same = (mine[:, None] == mine[None, :]) & (order[None, :] < order[:, None])
    rank = jnp.sum(same.astype(jnp.int32), axis=1)
    target = mine * cap + rank
    onehot = (target[:, None] == jnp.arange(slots, dtype=jnp.int32)[None, :]).astype(jnp.float32)
    outgoing = lax.dot_general(
        onehot,
        payload,
        (((0,), (1,)), ((), ())),
        precision=lax.Precision.HIGHEST,
        preferred_element_type=jnp.float32,
    )
    arrived = lax.all_to_all(
        outgoing.reshape(ndev, cap * 4 * levels),
        ("sec", "blk"),
        split_axis=0,
        concat_axis=0,
        tiled=True,
    )
    arrived = arrived.reshape(slots, 4, levels)
    tend_temp, tend_moist = condense(
        arrived[:, 0], arrived[:, 1], arrived[:, 2], arrived[:, 3], crm_state, phase_mask
    )
    tends = jnp.stack([tend_temp, tend_moist], axis=1)
    returned = lax.all_to_all(
        tends.reshape(ndev, cap * 2 * levels),
        ("sec", "blk"),
        split_axis=0,
        concat_axis=0,
        tiled=True,
    )
    returned = returned.reshape(slots, 2 * levels)
    column_tend = jnp.dot(
        onehot, returned, precision=lax.Precision.HIGHEST, preferred_element_type=jnp.float32
    )
    column_tend = column_tend.T.reshape(2, levels, cdev)
    return state + dyn + column_tend


def solution(mesh):
    return jax.shard_map(
        local,
        mesh=mesh,
        in_specs=(
            P(None, None, ("sec", "blk")),
            P(None, ("sec", "blk")),
            P(("sec", "blk"), None),
            P(("sec", "blk"), None),
            P(("sec", "blk"), None),
        ),
        out_specs=P(None, None, ("sec", "blk")),
        check_vma=False,
    )
```

profile of v0, /device:TPU:1, one launch (start us, length us, event | category | flops | bytes accessed | tf_op | source)
XLA Modules:
  0.0 209.5 jit_solution(16924140543291684147)
XLA Ops:
  0.0 1.0 copy.42
  1.0 3.1 %collective-permute-start = (f32[2,72,8]{1,0,2:T(2,128)S(1)}, f32[2,72,8]{1,0,2:T(2,128)S(1)}, u32[]{:S(2)}, u32[]{:S(2)}) collective-permute-start(f32[2,72,8]{1,0,2:T(2,128)S(1)} %get-tuple-element.63), channel_id=1, source_target_pairs={{0,1},{1,2},{2,3},{3,4},{4,5},{5,6},{6,7},{7,8},{8,9},{9,10},{10,1... | collective-permute-start | bytes 13832 | tf_op jit(solution)/shard_map/ppermute | solution.py:17
  4.1 0.9 convert_reduce_fusion
  5.0 0.7 fusion.48
  5.7 0.7 add_select_fusion
  6.4 6.1 %copy.54 = s32[256,4608]{0,1:T(8,128)} copy(s32[256,4608]{1,0:T(8,128)} %param.11) | data formatting | bytes 9437184 | tf_op args[4]
  12.5 5.4 %broadcast_select_fusion = (f32[256,4608]{0,1:T(8,128)}, pred[256,4608]{0,1:T(8,128)(4,1)S(1)}) fusion(s32[256,4608]{0,1:T(8,128)} %copy.54), kind=kLoop, calls=%fused_computation.60 | loop fusion | flops 2359296 | bytes 10616832 | tf_op jit(solution)/shard_map/jit(_where)/select_n | solution.py:30
  17.9 0.1 pad_maximum_fusion
  18.0 0.7 gather_fusion.3
  18.7 0.1 copy.48
  18.8 0.8 gather_fusion.2
  19.6 0.1 copy.47
  19.6 0.8 gather_fusion.1
  20.4 0.1 copy.46
  20.5 0.8 gather_fusion
  21.2 0.1 copy.45
  21.3 0.0 copy-done.6
  21.4 0.4 fusion.42
  21.9 1.1 all_to_all.16
  23.0 10.2 %all-to-all-start = ((f32[128,1,576]{2,1,0:T(1,128)}), f32[128,1,576]{2,1,0:T(1,128)S(1)}, u32[]{:S(2)}, u32[]{:S(2)}) async-start(f32[128,1,576]{2,1,0:T(1,128)} %all_to_all.16), calls=%async_computation | async-start | bytes 655360 | tf_op jit(solution)/shard_map/all_to_all | solution.py:75
  33.2 2.8 %broadcast_select_fusion.1 = f32[256,4608]{0,1:T(8,128)} fusion(pred[256,4608]{0,1:T(8,128)(4,1)S(1)} %get-tuple-element.16), kind=kLoop, calls=%fused_computation.61 | loop fusion | flops 1179648 | bytes 5898240 | tf_op jit(solution)/shard_map/jit(_where)/select_n | solution.py:31
  36.0 6.6 %copy.52 = bf16[256,9216]{0,1:T(8,128)(2,1)} copy(bf16[256,9216]{1,0:T(8,128)(2,1)} %param.10) | data formatting | bytes 9437184 | tf_op args[3]
  42.7 7.3 %convert.1 = f32[256,2,72,64]{0,3,2,1:T(8,128)} convert(bf16[256,2,72,64]{0,3,2,1:T(8,128)(2,1)} %bitcast.78) | non-fusion elementwise | flops 2359296 | bytes 14155776 | tf_op jit(solution)/shard_map/reshape | solution.py:26
  49.9 0.8 reduce
  50.7 0.5 reshape.82
  51.2 0.4 slice_multiply_fusion
  51.6 0.1 copy.61
  51.7 0.1 copy.62
  51.8 5.3 %fusion = (f32[256,72,64]{0,2,1:T(8,128)S(1)}, f32[256,72,64]{0,2,1:T(8,128)S(1)}) fusion(f32[256,2,72,64]{0,3,2,1:T(8,128)} %convert.1, f32[256,72]{0,1:T(8,128)S(1)} %bitcast.80, f32[256,72]{0,1:T(8,128)S(1)} %bitcast.81), kind=kLoop, calls=%fused_computation.5 | loop fusion | flops 2359296 | bytes 19021824 | tf_op jit(solution)/shard_map/add | solution.py:28
  57.2 0.1 fusion.65
  57.3 5.0 %fusion.66 = (f32[256,72,63]{0,2,1:T(8,128)}, f32[256,72,63]{0,2,1:T(8,128)}) fusion(f32[256,72,64]{0,2,1:T(8,128)S(1)} %get-tuple-element.25), kind=kLoop, calls=%fused_computation.116 | loop fusion | bytes 18579456 | tf_op jit(solution)/shard_map/jit(_roll_static)/slice | solution.py:35
  62.3 0.1 fusion.67
  62.4 1.2 copy-done.5
  63.6 4.7 %fusion.68 = (f32[256,72,63]{0,2,1:T(8,128)}, f32[256,72,63]{0,2,1:T(8,128)}) fusion(f32[256,72,64]{0,2,1:T(8,128)S(1)} %get-tuple-element.26), kind=kLoop, calls=%fused_computation.118 | loop fusion | bytes 18579456 | tf_op jit(solution)/shard_map/jit(_roll_static)/slice | solution.py:33
  68.3 0.1 copy.56
  68.3 0.1 copy.53
  68.4 18.1 %multiply_add_fusion.2 = (f32[256,72,64]{0,2,1:T(8,128)S(1)}, f32[256,72,64]{0,2,1:T(8,128)}, f32[256,72,64]{0,2,1:T(8,128)}) fusion(f32[256,72,64]{0,2,1:T(8,128)} %bitcast.72, f32[256,72,64]{0,2,1:T(8,128)} %bitcast.63, f32[256,72]{0,1:T(8,128)S(1)} %copy.53, f32[256,72,64]{0,2,1:T(8,128)} %copy-done.5, f32[256,72,1]{0,2,1:T(1,128)S(1)} %get-tuple-element.56, ...), kind=kLoop, calls=%fused_computation.55 | loop fusion | flops 27131904 | bytes 52051968 | tf_op jit(solution)/shard_map/add | solution.py:42
  86.5 5.4 %fusion.34 = f32[256,72,64]{0,2,1:T(8,128)S(1)} fusion(f32[256,72,64]{0,2,1:T(8,128)} %get-tuple-element.14, f32[256,72,64]{0,2,1:T(8,128)S(1)} %bitcast.66, f32[256,72,64]{0,2,1:T(8,128)} %get-tuple-element.13), kind=kLoop, calls=%fused_computation.57 | loop fusion | flops 7077888 | bytes 18874368 | tf_op jit(solution)/shard_map/sub | solution.py:41
  92.0 0.1 fusion.61
  92.1 5.0 %fusion.62 = (f32[256,72,63]{0,2,1:T(8,128)}, f32[256,72,63]{0,2,1:T(8,128)}) fusion(f32[256,72,64]{0,2,1:T(8,128)S(1)} %fusion.34), kind=kLoop, calls=%fused_computation.112 | loop fusion | bytes 18579456 | tf_op jit(solution)/shard_map/jit(_roll_static)/slice | solution.py:35
  97.1 0.1 fusion.63
  97.2 4.7 %fusion.64 = (f32[256,72,63]{0,2,1:T(8,128)}, f32[256,72,63]{0,2,1:T(8,128)}) fusion(f32[256,72,64]{0,2,1:T(8,128)S(1)} %get-tuple-element.12), kind=kLoop, calls=%fused_computation.114 | loop fusion | bytes 18579456 | tf_op jit(solution)/shard_map/jit(_roll_static)/slice | solution.py:33
  101.9 13.7 %multiply_add_fusion.1 = (f32[256,72,64]{0,2,1:T(8,128)S(1)}, f32[256,72,64]{0,2,1:T(8,128)}) fusion(f32[256,72,64]{0,2,1:T(8,128)} %bitcast.73, f32[256,72,64]{0,2,1:T(8,128)S(1)} %bitcast.67, f32[256,72]{0,1:T(8,128)S(1)} %copy.53, f32[256,72,64]{0,2,1:T(8,128)S(1)} %get-tuple-element.12, f32[256,72,1]{0,2,1:T(1,128)S(1)} %get-tuple-element.48, ...), kind=kLoop, calls=%fused_computation.53 | loop fusion | flops 27131904 | bytes 47333376 | tf_op jit(solution)/shard_map/add | solution.py:42
  115.5 6.8 %fusion.35 = f32[256,72,64]{0,2,1:T(8,128)S(1)} fusion(f32[256,72,64]{0,2,1:T(8,128)} %get-tuple-element.11, f32[256,72,64]{0,2,1:T(8,128)S(1)} %bitcast.68, f32[256,72]{0,1:T(8,128)S(1)} %copy.53, f32[256,72,64]{0,2,1:T(8,128)S(1)} %get-tuple-element.12, f32[256,72,1]{0,2,1:T(1,128)S(1)} %get-tuple-element.48, f32[256,72,63]{0,2,1:T(8,128)} %get-tuple-element.50, ...), kind=kLoop, calls=%fused_computation.58 | loop fusion | flops 16515072 | bytes 28385280 | tf_op jit(solution)/shard_map/sub | solution.py:41
  122.4 2.2 %copy-done.2 = f32[256,72,64]{0,2,1:T(8,128)} copy-done((f32[256,72,64]{0,2,1:T(8,128)}, f32[256,72,64]{0,2,1:T(8,128)S(1)}, u32[]{:S(2)}) %copy-start.2) | copy-done | bytes 4718616
  124.5 0.1 fusion.57
  124.7 9.3 %fusion.58 = (f32[256,72,63]{0,2,1:T(8,128)}, f32[256,72,63]{0,2,1:T(8,128)}) fusion(f32[256,72,64]{0,2,1:T(8,128)} %copy-done.2), kind=kLoop, calls=%fused_computation.108 | loop fusion | bytes 18579456 | tf_op jit(solution)/shard_map/jit(_roll_static)/slice | solution.py:35
  133.9 0.1 fusion.59
  134.0 4.6 %fusion.60 = (f32[256,72,63]{0,2,1:T(8,128)}, f32[256,72,63]{0,2,1:T(8,128)}) fusion(f32[256,72,64]{0,2,1:T(8,128)S(1)} %get-tuple-element.10), kind=kLoop, calls=%fused_computation.110 | loop fusion | bytes 18579456 | tf_op jit(solution)/shard_map/jit(_roll_static)/slice | solution.py:33
  138.6 14.4 %multiply_add_fusion = (f32[256,72,64]{0,2,1:T(8,128)}, f32[256,72,64]{0,2,1:T(8,128)}) fusion(f32[256,72,64]{0,2,1:T(8,128)S(1)} %bitcast.76, f32[256,72,64]{0,2,1:T(8,128)S(1)} %bitcast.69, f32[256,72]{0,1:T(8,128)S(1)} %copy.53, f32[256,72,64]{0,2,1:T(8,128)S(1)} %get-tuple-element.10, f32[256,72,1]{0,2,1:T(1,128)S(1)} %get-tuple-element.40, ...), kind=kLoop, calls=%fused_computation.51 | loop fusion | flops 27131904 | bytes 47333376 | tf_op jit(solution)/shard_map/add | solution.py:42
  153.0 6.8 %fusion.36 = f32[256,72,64]{0,2,1:T(8,128)S(1)} fusion(f32[256,72,64]{0,2,1:T(8,128)} %get-tuple-element.9, f32[256,72,64]{0,2,1:T(8,128)S(1)} %bitcast.70, f32[256,72]{0,1:T(8,128)S(1)} %copy.53, f32[256,72,64]{0,2,1:T(8,128)S(1)} %get-tuple-element.10, f32[256,72,1]{0,2,1:T(1,128)S(1)} %get-tuple-element.40, f32[256,72,63]{0,2,1:T(8,128)} %get-tuple-element.42, ...), kind=kLoop, calls=%fused_computation.59 | loop fusion | flops 16515072 | bytes 28385280 | tf_op jit(solution)/shard_map/sub | solution.py:41
  159.9 2.2 %copy-done.1 = f32[256,72,64]{0,2,1:T(8,128)} copy-done((f32[256,72,64]{0,2,1:T(8,128)}, f32[256,72,64]{0,2,1:T(8,128)S(1)}, u32[]{:S(2)}) %copy-start.1) | copy-done | bytes 4718616
  162.0 0.1 fusion.56
  162.2 9.3 %fusion.55 = (f32[256,72,63]{0,2,1:T(8,128)}, f32[256,72,63]{0,2,1:T(8,128)}) fusion(f32[256,72,64]{0,2,1:T(8,128)} %copy-done.1), kind=kLoop, calls=%fused_computation.105 | loop fusion | bytes 18579456 | tf_op jit(solution)/shard_map/jit(_roll_static)/slice | solution.py:35
  171.5 0.1 fusion.53
  171.6 4.8 %fusion.54 = (f32[256,72,63]{0,2,1:T(8,128)}, f32[256,72,63]{0,2,1:T(8,128)}) fusion(f32[256,72,64]{0,2,1:T(8,128)S(1)} %copy-done), kind=kLoop, calls=%fused_computation.104 | loop fusion | bytes 18579456 | tf_op jit(solution)/shard_map/jit(_roll_static)/slice | solution.py:33
  176.3 10.9 %add_reduce_fusion = (f32[256,72]{0,1:T(8,128)S(1)}, f32[256,72]{0,1:T(8,128)S(1)}) fusion(f32[256,72,64]{0,2,1:T(8,128)S(1)} %bitcast.77, f32[256,72,64]{0,2,1:T(8,128)S(1)} %bitcast.71, f32[256,72]{0,1:T(8,128)S(1)} %copy.53, f32[256,72,64]{0,2,1:T(8,128)S(1)} %copy-done, f32[256,72,1]{0,2,1:T(1,128)S(1)} %get-tuple-element.28, ...), kind=kLoop, calls=%fused_computation.49 | loop fusion | flops 30633984 | bytes 38043648 | tf_op jit(solution)/shard_map/reduce_sum | solution.py:43
  187.3 0.1 copy.57
  187.5 0.4 all_to_all.17
  187.9 20.0 %all_to_all.20 = f32[128,1,288]{2,1,0:T(1,128)S(1)} all-to-all(f32[128,1,288]{2,1,0:T(1,128)S(1)} %all_to_all.17), channel_id=1, replica_groups=mesh['sec'=4,'blk'=32] {'sec','blk'}, dimensions={0} | all-to-all | bytes 294912 | tf_op jit(solution)/shard_map/all_to_all | solution.py:87
  207.9 0.5 reduce.1
  208.3 0.1 reshape.85
  208.4 0.1 copy.59
  208.5 0.9 convolution_add_fusion
  (33 shorter events, 0.2 us)
Async XLA Ops:
  1.0 16.9 %collective-permute-start = (f32[2,72,8]{1,0,2:T(2,128)S(1)}, f32[2,72,8]{1,0,2:T(2,128)S(1)}, u32[]{:S(2)}, u32[]{:S(2)}) collective-permute-start(f32[2,72,8]{1,0,2:T(2,128)S(1)} %get-tuple-element.63), channel_id=1, source_target_pairs={{0,1},{1,2},{2,3},{3,4},{4,5},{5,6},{6,7},{7,8},{8,9},{9,10},{10,1... | collective-permute-start | bytes 13832 | tf_op jit(solution)/shard_map/ppermute | solution.py:17
  4.1 13.8 %collective-permute-start.1 = (f32[2,72,8]{1,0,2:T(2,128)S(1)}, f32[2,72,8]{1,0,2:T(2,128)S(1)}, u32[]{:S(2)}, u32[]{:S(2)}) collective-permute-start(f32[2,72,8]{1,0,2:T(2,128)S(1)} %get-tuple-element.64), channel_id=1, source_target_pairs={{1,0},{2,1},{3,2},{4,3},{5,4},{6,5},{7,6},{8,7},{9,8},{10,9},{11,1... | collective-permute-start | bytes 13832 | tf_op jit(solution)/shard_map/ppermute | solution.py:18
  12.5 8.9 %copy-start.6 = (f32[2,72,128]{2,1,0:T(8,128)S(1)}, f32[2,72,128]{2,1,0:T(8,128)}, u32[]{:S(2)}) copy-start(f32[2,72,128]{2,1,0:T(8,128)} %param.7) | copy-start | bytes 221188
  23.0 26.9 %all-to-all-start = ((f32[128,1,576]{2,1,0:T(1,128)}), f32[128,1,576]{2,1,0:T(1,128)S(1)}, u32[]{:S(2)}, u32[]{:S(2)}) async-start(f32[128,1,576]{2,1,0:T(1,128)} %all_to_all.16), calls=%async_computation | async-start | bytes 655360 | tf_op jit(solution)/shard_map/all_to_all | solution.py:75
  57.2 5.1 %copy-start.4 = (f32[256,72,64]{0,2,1:T(8,128)}, f32[256,72,64]{0,2,1:T(8,128)S(1)}, u32[]{:S(2)}) copy-start(f32[256,72,64]{0,2,1:T(8,128)S(1)} %get-tuple-element.25) | copy-start | bytes 14155780
  57.2 6.4 %copy-start.5 = (f32[256,72,64]{0,2,1:T(8,128)}, f32[256,72,64]{0,2,1:T(8,128)S(1)}, u32[]{:S(2)}) copy-start(f32[256,72,64]{0,2,1:T(8,128)S(1)} %get-tuple-element.26) | copy-start | bytes 14155780
  63.6 22.9 %slice-start = ((s8[4718592]{0:T(1024)(128)(4,1)}), s8[524288]{0:T(1024)(128)(4,1)S(1)}, s32[]{:S(2)}) async-start(s8[4718592]{0:T(1024)(128)(4,1)} %bitcast.64), calls=%async_computation.2 | async-start | bytes 1048576
  68.4 18.1 %slice-start.1 = ((s8[4718592]{0:T(1024)(128)(4,1)}), s8[4194304]{0:T(1024)(128)(4,1)S(1)}, s32[]{:S(2)}) async-start(s8[4718592]{0:T(1024)(128)(4,1)} %bitcast.64), calls=%async_computation.3 | async-start | bytes 8388608
  92.0 5.1 %copy-start.3 = (f32[256,72,64]{0,2,1:T(8,128)}, f32[256,72,64]{0,2,1:T(8,128)S(1)}, u32[]{:S(2)}) copy-start(f32[256,72,64]{0,2,1:T(8,128)S(1)} %fusion.34) | copy-start | bytes 14155780
  122.4 2.2 %copy-start.2 = (f32[256,72,64]{0,2,1:T(8,128)}, f32[256,72,64]{0,2,1:T(8,128)S(1)}, u32[]{:S(2)}) copy-start(f32[256,72,64]{0,2,1:T(8,128)S(1)} %fusion.35) | copy-start | bytes 14155780
  124.7 14.0 %slice-start.2 = ((s8[4718592]{0:T(1024)(128)(4,1)}), s8[4194304]{0:T(1024)(128)(4,1)S(1)}, s32[]{:S(2)}) async-start(s8[4718592]{0:T(1024)(128)(4,1)} %bitcast.74), calls=%async_computation.4 | async-start | bytes 8388608
  133.9 4.7 %slice-start.3 = ((s8[4718592]{0:T(1024)(128)(4,1)}), s8[524288]{0:T(1024)(128)(4,1)S(1)}, s32[]{:S(2)}) async-start(s8[4718592]{0:T(1024)(128)(4,1)} %bitcast.74), calls=%async_computation.5 | async-start | bytes 1048576
  159.9 2.2 %copy-start.1 = (f32[256,72,64]{0,2,1:T(8,128)}, f32[256,72,64]{0,2,1:T(8,128)S(1)}, u32[]{:S(2)}) copy-start(f32[256,72,64]{0,2,1:T(8,128)S(1)} %fusion.36) | copy-start | bytes 14155780
  162.2 9.3 %copy-start = (f32[256,72,64]{0,2,1:T(8,128)S(1)}, f32[256,72,64]{0,2,1:T(8,128)}, u32[]{:S(2)}) copy-start(f32[256,72,64]{0,2,1:T(8,128)} %get-tuple-element.8) | copy-start | bytes 14155780
where the time goes:
time: 210 us; the launch traced here: 209 us
  other arithmetic  101 us (48%)
  local copies, waits for them, and re-layouts  73.4 us (35%)
  blocking collectives  20 us (10%)
  starting transfers between devices  13.3 us (6%)
    add x3, other arithmetic, condense(): temper = temper + heat * cond  46.1 us
    all_to_all x1, blocking collectives, local(): lax.all_to_all(tends.reshape(ndev, cap * 2 * levels), ('sec', 'blk'), spl...  20 us
    slice x6, local copies, waits for them, and re-layouts, condense(): jnp.roll(moisture, 1, 2) + jnp.roll(moisture, -1, 2) - 2.0 * moisture  19.6 us
    unnamed x27, local copies, waits for them, and re-layouts  19.4 us
    sub x3, other arithmetic, condense(): moisture = moisture - cond  19.1 us
    slice x8, local copies, waits for them, and re-layouts, condense(): jnp.roll(temper, 1, 2) + jnp.roll(temper, -1, 2) - 2.0 * temper  19.1 us
    reduce_sum x1, other arithmetic, condense(): jnp.mean(temper, axis=2) - temp_col  10.9 us
    all_to_all x1, starting transfers between devices, local(): lax.all_to_all(outgoing.reshape(ndev, cap * 4 * levels), ('sec', 'blk'),...  10.2 us
  transfers between devices with their start and end apart: 3, of which 0 were waited for; matrix products, arithmetic and copies ran while one was open for 15% of the time, Pallas kernels for 0%

commit v1 on v0

v1 whole, which is shorter than its diff:
```python
import functools
import math

import jax
import jax.numpy as jnp
from jax import lax
from jax.experimental import pallas as pl
from jax.experimental.pallas import tpu as pltpu

SUB = 4
REACH = 8
F32 = jnp.float32
BF16 = jnp.bfloat16
MESH = pl.DeviceIdType.MESH

GROW = [5.0 ** k for k in range(SUB + 1)]
SHIFT = [GROW[k] * (math.log(0.8) + k * math.log(5.0)) / 0.3 for k in range(SUB + 1)]
EXPO = [0.3 * math.log2(math.e) / GROW[k] for k in range(SUB + 1)]


def nt(a, b):
    return lax.dot_general(a, b, (((1,), (1,)), ((), ())), preferred_element_type=F32)


def nn(a, b):
    return lax.dot_general(a, b, (((1,), (0,)), ((), ())), preferred_element_type=F32)


def halves(a):
    high = a.astype(BF16)
    return high, (a - high.astype(F32)).astype(BF16)


def iota(shape, dim):
    return lax.broadcasted_iota(jnp.int32, shape, dim)


def unit(wt, wm, ra, ga, base, quad, lane):
    lanes = pl.ds(lane * 128, 128)
    turn = lambda v: pltpu.roll(v, 4, axis=0)
    tcol, mcol = base[0, quad, :, lanes], base[1, quad, :, lanes]
    tforce, mforce = base[2, quad, :, lanes], base[3, quad, :, lanes]
    tadd = [None] + [tforce * (GROW[k] / SUB) + (SHIFT[k] - (5.0 * SHIFT[k - 1] if k > 1 else 0.0)) for k in range(1, SUB + 1)]
    madd = [None] + [mforce * (GROW[k] / SUB) for k in range(1, SUB + 1)]
    tadd[1] = tadd[1] + 5.0 * tcol
    madd[1] = madd[1] + 5.0 * mcol
    rate, gain = {}, {}

    def coeffs(j):
        if j not in rate:
            if j < 32:
                rate[j] = ra[quad, j * 8:j * 8 + 8, lanes]
                gain[j] = ga[quad, j * 8:j * 8 + 8, lanes]
            else:
                rate[j] = turn(ra[quad, (j - 32) * 8:(j - 32) * 8 + 8, lanes])
                gain[j] = turn(ga[quad, (j - 32) * 8:(j - 32) * 8 + 8, lanes])
        return rate[j], gain[j]

    temps = [{} for _ in range(SUB + 1)]
    moists = [{} for _ in range(SUB + 1)]
    tpair = [{} for _ in range(SUB + 1)]
    mpair = [{} for _ in range(SUB + 1)]
    total_t, total_m = [], []

    def condense(k, j, t, m):
        r, g = coeffs(j)
        pos = jnp.maximum(m - jnp.exp2(t * EXPO[k]), 0.0)
        temps[k][j] = t + g * pos
        moists[k][j] = m - r * pos

    def get(store, k, j):
        if j not in store[k]:
            store[k][j] = turn(store[k][j - 32])
        return store[k][j]

    def pair(store, pairs, k, j):
        if j not in pairs[k]:
            pairs[k][j] = get(store, k, j - 1) + get(store, k, j)
        return pairs[k][j]

    def spread(store, pairs, k, j):
        return (pair(store, pairs, k, j) + get(store, k, j)) + pair(store, pairs, k, j + 1)

    for step in range(32 + 2 * SUB):
        if step < 32:
            rows = slice(step * 8, step * 8 + 8)
            condense(1, step, wt[quad, rows, lanes] + tadd[1], wm[quad, rows, lanes] + madd[1])
        for k in range(2, SUB + 1):
            j = step - (k - 1)
            if k - 1 <= j < k - 1 + 32:
                t = spread(temps, tpair, k - 1, j) + tadd[k]
                m = spread(moists, mpair, k - 1, j) + madd[k]
                condense(k, j, t, m)
                if k == SUB:
                    total_t.append(temps[k][j])
                    total_m.append(moists[k][j])
                    if len(total_t) > 4:
                        total_t = total_t[1:4] + [total_t[0] + total_t[4]]
                        total_m = total_m[1:4] + [total_m[0] + total_m[4]]
    sum_t = (total_t[0] + total_t[1]) + (total_t[2] + total_t[3])
    sum_m = (total_m[0] + total_m[1]) + (total_m[2] + total_m[3])
    sum_t = sum_t + turn(sum_t)
    sum_m = sum_m + turn(sum_m)
    tend_t = (sum_t * (1.0 / 64) - SHIFT[SUB]) * (1.0 / GROW[SUB]) - tcol
    tend_m = (sum_m * (1.0 / 64)) * (1.0 / GROW[SUB]) - mcol
    return tend_t, tend_m


def kernel(nblk, ndev, state, nbr, own, crm, mask, out,
           ct, cm, mk, wt, wm, ra, ga, base, sp, dyn, hot, edge, halo, send, arr, tend, tmp, rsend, rarr,
           csem, halo_send, halo_recv, send_sem, recv_sem, rsend_sem, rrecv_sem, own_sem, rown_sem):
    me = lax.axis_index("sec") * nblk + lax.axis_index("blk")
    right, left = lax.rem(me + 1, ndev), lax.rem(me + ndev - 1, ndev)
    at = lambda d: (d // nblk, lax.rem(d, nblk))
    octs = 9

    def loads(o):
        cols = pl.ds(pl.multiple_of(o * 512, 512), 512)
        mcols = pl.ds(pl.multiple_of(4608 + o * 512, 512), 512)
        return [
            pltpu.make_async_copy(crm.at[:, cols], ct.at[o], csem.at[0, o]),
            pltpu.make_async_copy(crm.at[:, mcols], cm.at[o], csem.at[1, o]),
            pltpu.make_async_copy(mask.at[:, cols], mk.at[o], csem.at[2, o]),
        ]

    barrier = pltpu.get_barrier_semaphore()

    @pl.loop(1, ndev)
    def _(k):
        pl.semaphore_signal(barrier, inc=1, device_id=at(lax.rem(me + k, ndev)), device_id_type=MESH)

    @pl.loop(0, octs)
    def _(o):
        for copy in loads(o):
            copy.start()

    sp[...] = jnp.zeros_like(sp)
    sp[0:72, :] = state[0]
    sp[128:200, :] = state[1]
    st = sp[...]
    sh, sm = halves(st)
    pick_row, pick_col = iota((16, 128), 0), iota((16, 128), 1)
    pick = jnp.where(pick_col == jnp.where(pick_row < 8, pick_row, pick_row + 112), 1.0, 0.0).astype(BF16)
    edge[...] = nt(pick, sh) + nt(pick, sm)
    halo[16:, :] = jnp.zeros((112, 256), F32)

    pl.semaphore_wait(barrier, ndev - 1)
    to_left = pltpu.make_async_remote_copy(
        src_ref=edge.at[0:8], dst_ref=halo.at[8:16], send_sem=halo_send.at[0], recv_sem=halo_recv.at[0],
        device_id=at(left), device_id_type=MESH)
    to_right = pltpu.make_async_remote_copy(
        src_ref=edge.at[8:16], dst_ref=halo.at[0:8], send_sem=halo_send.at[1], recv_sem=halo_recv.at[1],
        device_id=at(right), device_id_type=MESH)
    to_left.start()
    to_right.start()

    row, col = iota((128, 128), 0), iota((128, 128), 1)
    own_down = jnp.broadcast_to(own[...], (128, 128))
    own_across = jnp.sum(jnp.where(row == col, own_down, 0), axis=0, keepdims=True)
    rank = jnp.sum(jnp.where((own_down == own_across) & (row < col), 1, 0), axis=0, keepdims=True)
    for r in range(2):
        hot[r * 128:(r + 1) * 128, :] = jnp.where((row == own_across) & (rank == r), 1.0, 0.0).astype(BF16)
    place = nbr[...] - (me * 128 - REACH)
    place = jnp.where(place < 0, place + ndev * 128, place)
    place = jnp.where(place >= ndev * 128, place - ndev * 128, place)
    inner = jnp.where(row == col, -4.0, 0.0)
    outer = jnp.zeros((128, 128), F32)
    far = jnp.where(row < 8, row, row + 128)
    for k in range(4):
        p = place[k:k + 1, :]
        inner = inner + jnp.where(p == row + REACH, 1.0, 0.0)
        outer = outer + jnp.where((p == far) & (row < 16), 1.0, 0.0)
    inner, outer = inner.astype(BF16), outer.astype(BF16)
    near = nn(sh, inner) + nn(sm, inner)
    mrow, mcol = iota((256, 256), 0), iota((256, 256), 1)
    same = (mrow % 4) == (mcol // 64)
    gap = (mcol % 64 - (((mrow % 8) // 4) * 32 + mrow // 8)) % 64
    move = jnp.where(same & (gap == 0), 1.0, 0.0).astype(BF16)
    mix = jnp.where(same & (gap == 0), 3.0, jnp.where(same & ((gap == 1) | (gap == 63)), 1.0, 0.0)).astype(BF16)

    to_left.wait()
    to_right.wait()
    hh, hm = halves(jnp.concatenate([jnp.transpose(halo[:, 0:128]), jnp.transpose(halo[:, 128:256])], axis=0))
    dyn[...] = 0.15 * (near + (nn(hh, outer) + nn(hm, outer)))
    dh, dm = halves(dyn[...])
    hots = hot[...]
    for f in range(4):
        high, mid = ((sh, sm), (dh, dm))[f // 2]
        part = slice((f % 2) * 128, (f % 2) * 128 + 128)
        rows = nt(hots, high[part]) + nt(hots, mid[part])
        for r in range(2):
            send[pl.ds(r * 4 + f, 128, stride=8), :] = rows[r * 128:(r + 1) * 128]

    block = lambda ref, d, n: ref.at[pl.ds(pl.multiple_of(d * 8, 8), n)]

    def scatter(d):
        return pltpu.make_async_remote_copy(
            src_ref=block(send, d, 8), dst_ref=block(arr, me, 8), send_sem=send_sem, recv_sem=recv_sem,
            device_id=at(d), device_id_type=MESH)

    @pl.loop(1, ndev)
    def _(k):
        scatter(lax.rem(me + k, ndev)).start()

    mine = pltpu.make_async_copy(block(send, me, 8), block(arr, me, 8), own_sem)
    mine.start()

    @pl.loop(0, octs)
    def _(o):
        for copy in loads(o):
            copy.wait()
        for half in range(2):
            quad = o * 2 + half
            lanes = slice(half * 256, half * 256 + 256)
            wt[quad] = nt(mix, ct[o, :, lanes])
            wm[quad] = nt(mix, cm[o, :, lanes])
            ice = nt(move, mk[o, :, lanes].astype(F32).astype(BF16)) > 0.5
            ra[quad] = jnp.where(ice, 0.3, 0.7)
            ga[quad] = jnp.where(ice, 0.39, 0.7)

    everyone = pl.ds(0, (ndev - 1) * 8)
    whole = pltpu.make_async_remote_copy(
        src_ref=send.at[everyone], dst_ref=arr.at[everyone], send_sem=send_sem, recv_sem=recv_sem,
        device_id=at(right), device_id_type=MESH)
    whole.wait_recv()
    mine.wait()

    drow, dcol = iota((144, 128), 0), iota((144, 128), 1)
    twice = jnp.where(dcol == (drow // 8) * 4 + drow % 4, 1.0, 0.0).astype(BF16)
    for f in range(4):
        high, mid = halves(arr[pl.ds(f, 256, stride=4), :])
        base[f] = (nt(twice, high) + nt(twice, mid)).reshape(18, 8, 256)

    upper = iota((8, 128), 0) < 4

    def giveback(d):
        return pltpu.make_async_remote_copy(
            src_ref=block(rsend, d, 4), dst_ref=block(rarr, me, 4), send_sem=rsend_sem, recv_sem=rrecv_sem,
            device_id=at(d), device_id_type=MESH)

    for h in range(2):
        @pl.loop(0, octs)
        def _(o, h=h):
            ta, ma = unit(wt, wm, ra, ga, base, o * 2, h)
            tb, mb = unit(wt, wm, ra, ga, base, o * 2 + 1, h)
            tend[h, 0, pl.ds(pl.multiple_of(o * 8, 8), 8), :] = jnp.where(upper, ta, tb)
            tend[h, 1, pl.ds(pl.multiple_of(o * 8, 8), 8), :] = jnp.where(upper, ma, mb)

        for f in range(2):
            tmp[...] = jnp.transpose(tend[h, f])
            for r in range(2):
                rsend[pl.ds(h * 512 + r * 2 + f, 64, stride=8), :] = tmp[pl.ds(r, 64, stride=2), :]

        @pl.loop(0, 64)
        def _(k, h=h):
            d = h * 64 + lax.rem(me + k, 64)

            @pl.when(d != me)
            def _():
                giveback(d).start()

    mine_back = pltpu.make_async_copy(block(rsend, me, 4), block(rarr, me, 4), rown_sem)
    mine_back.start()
    settled = sp[...] + dyn[...]
    back = pl.ds(0, (ndev - 1) * 4)
    whole_back = pltpu.make_async_remote_copy(
        src_ref=rsend.at[back], dst_ref=rarr.at[back], send_sem=rsend_sem, recv_sem=rrecv_sem,
        device_id=at(right), device_id_type=MESH)
    whole_back.wait_recv()
    mine_back.wait()
    for f in range(2):
        moved = jnp.zeros((128, 128), F32)
        for r in range(2):
            high, mid = halves(jnp.transpose(rarr[pl.ds(r * 2 + f, 128, stride=8), :]))
            take = hots[r * 128:(r + 1) * 128]
            moved = moved + (nn(high, take) + nn(mid, take))
        out[f] = settled[f * 128:f * 128 + 72] + moved[0:72]
    whole.wait_send()
    whole_back.wait_send()


def solution(mesh):
    nsec, nblk = mesh.shape["sec"], mesh.shape["blk"]
    ndev = nsec * nblk
    vmem = pl.BlockSpec(memory_space=pltpu.VMEM)
    hbm = pl.BlockSpec(memory_space=pl.ANY)
    dma = pltpu.SemaphoreType.DMA

    call = pl.pallas_call(
        functools.partial(kernel, nblk, ndev),
        out_shape=jax.ShapeDtypeStruct((2, 72, 128), F32),
        in_specs=[vmem, vmem, vmem, hbm, hbm],
        out_specs=vmem,
        scratch_shapes=[
            pltpu.VMEM((9, 256, 512), BF16),
            pltpu.VMEM((9, 256, 512), BF16),
            pltpu.VMEM((9, 256, 512), jnp.int32),
            pltpu.VMEM((18, 256, 256), F32),
            pltpu.VMEM((18, 256, 256), F32),
            pltpu.VMEM((18, 256, 256), F32),
            pltpu.VMEM((18, 256, 256), F32),
            pltpu.VMEM((4, 18, 8, 256), F32),
            pltpu.VMEM((256, 128), F32),
            pltpu.VMEM((256, 128), F32),
            pltpu.VMEM((256, 128), BF16),
            pltpu.VMEM((16, 256), F32),
            pltpu.VMEM((128, 256), F32),
            pltpu.VMEM((1024, 128), F32),
            pltpu.VMEM((1024, 128), F32),
            pltpu.VMEM((2, 2, 128, 128), F32),
            pltpu.VMEM((128, 128), F32),
            pltpu.VMEM((1024, 128), F32),
            pltpu.VMEM((1024, 128), F32),
            dma((3, 9)), dma((2,)), dma((2,)), dma, dma, dma, dma, dma, dma,
        ],
        compiler_params=pltpu.CompilerParams(
            collective_id=0, has_side_effects=True, vmem_limit_bytes=56 * 2**20),
        name="gcm_step",
    )

    def local(state, neighbors, owner, crm_state, phase_mask):
        return call(state, neighbors, owner, crm_state, phase_mask)

    both = ("sec", "blk")
    P = jax.sharding.PartitionSpec
    return jax.shard_map(
        local,
        mesh=mesh,
        in_specs=(P(None, None, both), P(None, both), P(both, None), P(both, None), P(both, None)),
        out_specs=P(None, None, both),
        check_vma=False,
    )
```

time: 210 us -> 47.6 us (0.23)
  the two profiles are of different devices: /device:TPU:1 before, /device:TPU:7 now
where the time goes in v1:
time: 47.6 us; the launch traced here: 47.4 us
  Pallas kernels  44.5 us (93%)
  local copies, waits for them, and re-layouts  2.91 us (6%)
    pallas_call x1, Pallas kernels, local(): return call(state, neighbors, owner, crm_state, phase_mask)  44.5 us
    unnamed x2, local copies, waits for them, and re-layouts  2.91 us

profile of v1, /device:TPU:7, one launch (start us, length us, event | category | flops | bytes accessed | tf_op | source)
XLA Modules:
  0.0 47.4 jit_solution(10655272155091544322)
XLA Ops:
  0.0 1.4 %copy.6.own = s32[128,1]{1,0:T(8,128)} copy(s32[128,1]{0,1:T(1,128)} %param.7) | data formatting | bytes 1024 | tf_op args[2]
  1.4 44.5 %gcm_step.1 = f32[2,72,128]{2,1,0:T(8,128)} custom-call(f32[2,72,128]{2,1,0:T(8,128)} %state.1, s32[4,128]{1,0:T(4,128)} %nbr.1, s32[128,1]{1,0:T(8,128)} %copy.6.own, bf16[256,9216]{1,0:T(8,128)(2,1)} %crm.1, s32[256,4608]{1,0:T(8,128)} %mask.1), custom_call_target="tpu_custom_call" | custom-call | tf_op jit(solution)/shard_map/gcm_step/pallas_call | solution.py:322
  45.9 1.5 %copy.8 = f32[2,72,128]{2,1,0:T(8,128)} copy(f32[2,72,128]{2,1,0:T(8,128)} %gcm_step.1) | data formatting | bytes 147456

commit v2 on v1

v2 whole, which is shorter than its diff:
```python
import functools
import math

import jax
import jax.numpy as jnp
from jax import lax
from jax.experimental import pallas as pl
from jax.experimental.pallas import tpu as pltpu

SUB = 4
REACH = 8
F32 = jnp.float32
BF16 = jnp.bfloat16
MESH = pl.DeviceIdType.MESH

GROW = [5.0 ** k for k in range(SUB + 1)]
SHIFT = [GROW[k] * (math.log(0.8) + k * math.log(5.0)) / 0.3 for k in range(SUB + 1)]
EXPO = [0.3 * math.log2(math.e) / GROW[k] for k in range(SUB + 1)]


def nt(a, b):
    return lax.dot_general(a, b, (((1,), (1,)), ((), ())), preferred_element_type=F32)


def nn(a, b):
    return lax.dot_general(a, b, (((1,), (0,)), ((), ())), preferred_element_type=F32)


def halves(a, dim):
    high = a.astype(BF16)
    return jnp.concatenate([high, (a - high.astype(F32)).astype(BF16)], axis=dim)


def iota(shape, dim):
    return lax.broadcasted_iota(jnp.int32, shape, dim)


def turn(v):
    return pltpu.roll(v, 4, axis=0)


def unit(wt, wm, ra, ga, column, quad, lane):
    lanes = pl.ds(lane * 128, 128)
    tcol, mcol, tforce, mforce = column
    tadd = [None] + [tforce * (GROW[k] / SUB) + (SHIFT[k] - (5.0 * SHIFT[k - 1] if k > 1 else 0.0)) for k in range(1, SUB + 1)]
    madd = [None] + [mforce * (GROW[k] / SUB) for k in range(1, SUB + 1)]
    tadd[1] = tadd[1] + 5.0 * tcol
    madd[1] = madd[1] + 5.0 * mcol
    rate, gain = {}, {}

    def coeffs(j):
        if j not in rate:
            rows = slice((j % 32) * 8, (j % 32) * 8 + 8)
            rate[j], gain[j] = ra[quad, rows, lanes], ga[quad, rows, lanes]
            if j >= 32:
                rate[j], gain[j] = turn(rate[j]), turn(gain[j])
        return rate[j], gain[j]

    temps = [{} for _ in range(SUB + 1)]
    moists = [{} for _ in range(SUB + 1)]
    tpair = [{} for _ in range(SUB + 1)]
    mpair = [{} for _ in range(SUB + 1)]
    total_t, total_m = [], []

    def condense(k, j, t, m):
        r, g = coeffs(j)
        pos = jnp.maximum(m - jnp.exp2(t * EXPO[k]), 0.0)
        temps[k][j] = t + g * pos
        moists[k][j] = m - r * pos

    def get(store, k, j):
        if j not in store[k]:
            store[k][j] = turn(store[k][j - 32])
        return store[k][j]

    def pair(store, pairs, k, j):
        if j not in pairs[k]:
            pairs[k][j] = get(store, k, j - 1) + get(store, k, j)
        return pairs[k][j]

    def spread(store, pairs, k, j):
        return (pair(store, pairs, k, j) + get(store, k, j)) + pair(store, pairs, k, j + 1)

    for step in range(32 + 2 * SUB):
        if step < 32:
            rows = slice(step * 8, step * 8 + 8)
            condense(1, step, wt[quad, rows, lanes] + tadd[1], wm[quad, rows, lanes] + madd[1])
        for k in range(2, SUB + 1):
            j = step - (k - 1)
            if k - 1 <= j < k - 1 + 32:
                t = spread(temps, tpair, k - 1, j) + tadd[k]
                m = spread(moists, mpair, k - 1, j) + madd[k]
                condense(k, j, t, m)
                if k == SUB:
                    total_t.append(temps[k][j])
                    total_m.append(moists[k][j])
                    if len(total_t) > 4:
                        total_t = total_t[1:4] + [total_t[0] + total_t[4]]
                        total_m = total_m[1:4] + [total_m[0] + total_m[4]]
    sum_t = (total_t[0] + total_t[1]) + (total_t[2] + total_t[3])
    sum_m = (total_m[0] + total_m[1]) + (total_m[2] + total_m[3])
    sum_t = sum_t + turn(sum_t)
    sum_m = sum_m + turn(sum_m)
    return (sum_t * (1.0 / 64) - SHIFT[SUB]) * (1.0 / GROW[SUB]), (sum_m * (1.0 / 64)) * (1.0 / GROW[SUB])


def kernel(nblk, ndev, state, nbr, own, crm, mask, out,
           st, nb, ow, ct, cm, mk, wt, wm, ra, ga, feat, near, sq, edge, halo, send, arr, first, tend, tmp, tail, rsend, rarr,
           isem, csem, halo_send, halo_recv, send_sem, recv_sem, rsend_sem, rrecv_sem, own_sem, rown_sem):
    me = lax.axis_index("sec") * nblk + lax.axis_index("blk")
    right, left = lax.rem(me + 1, ndev), lax.rem(me + ndev - 1, ndev)
    at = lambda d: (d // nblk, lax.rem(d, nblk))
    octs = 9

    small = [pltpu.make_async_copy(state, st, isem.at[0]), pltpu.make_async_copy(nbr, nb, isem.at[1]),
             pltpu.make_async_copy(own, ow, isem.at[2])]
    for copy in small:
        copy.start()
    barrier = pltpu.get_barrier_semaphore()

    @pl.loop(1, ndev)
    def _(k):
        pl.semaphore_signal(barrier, inc=1, device_id=at(lax.rem(me + k, ndev)), device_id_type=MESH)

    def loads(o):
        cols = pl.ds(pl.multiple_of(o * 512, 512), 512)
        mcols = pl.ds(pl.multiple_of(4608 + o * 512, 512), 512)
        return [
            pltpu.make_async_copy(crm.at[:, cols], ct.at[o], csem.at[0, o]),
            pltpu.make_async_copy(crm.at[:, mcols], cm.at[o], csem.at[1, o]),
            pltpu.make_async_copy(mask.at[:, cols], mk.at[o], csem.at[2, o]),
        ]

    for copy in small:
        copy.wait()

    @pl.loop(0, octs)
    def _(o):
        for copy in loads(o):
            copy.start()

    sq[0:16, :] = jnp.zeros((16, 128), F32)
    sq[16:160, :] = st[...]
    sq[160:256, :] = jnp.zeros((96, 128), F32)
    pick_row, pick_col = iota((16, 128), 0), iota((16, 128), 1)
    pick = jnp.where(pick_col == jnp.where(pick_row < 8, pick_row, pick_row + 112), 1.0, 0.0).astype(BF16)
    edge[...] = nt(jnp.concatenate([pick, pick], axis=1), halves(sq[...], 1))

    pl.semaphore_wait(barrier, ndev - 1)
    to_left = pltpu.make_async_remote_copy(
        src_ref=edge.at[0:8], dst_ref=halo.at[8:16], send_sem=halo_send.at[0], recv_sem=halo_recv.at[0],
        device_id=at(left), device_id_type=MESH)
    to_right = pltpu.make_async_remote_copy(
        src_ref=edge.at[8:16], dst_ref=halo.at[0:8], send_sem=halo_send.at[1], recv_sem=halo_recv.at[1],
        device_id=at(right), device_id_type=MESH)
    to_left.start()
    to_right.start()

    row, col = iota((128, 128), 0), iota((128, 128), 1)
    own_across = ow[...]
    own_down = jnp.sum(jnp.where(row == col, own_across, 0), axis=1, keepdims=True)
    rank = jnp.sum(jnp.where((own_down == own_across) & (row < col), 1, 0), axis=0, keepdims=True)
    hot = jnp.concatenate(
        [jnp.where((row == own_across) & (rank == r), 1.0, 0.0).astype(BF16) for r in range(2)], axis=0)
    place = nb[...] - (me * 128 - REACH)
    place = jnp.where(place < 0, place + ndev * 128, place)
    place = jnp.where(place >= ndev * 128, place - ndev * 128, place)
    inner = jnp.where(row == col, -4.0, 0.0)
    halo_row = iota((16, 128), 0)
    halo_place = jnp.where(halo_row < 8, halo_row, halo_row + 128)
    outer = jnp.zeros((16, 128), F32)
    for k in range(4):
        p = place[k:k + 1, :]
        inner = inner + jnp.where(p == row + REACH, 1.0, 0.0)
        outer = outer + jnp.where(p == halo_place, 1.0, 0.0)
    inner, outer = inner.astype(BF16), outer.astype(BF16)
    near[...] = 0.15 * nn(halves(st[...], 1), jnp.concatenate([inner, inner], axis=0))
    hot_twice = jnp.concatenate([hot, hot], axis=1)
    rows = nt(hot_twice, jnp.concatenate([halves(st[...], 1), halves(near[...], 1)], axis=0))
    for r in range(2):
        send[pl.ds(r * 2, 128, stride=8), :] = rows[r * 128:(r + 1) * 128, 0:128]
    first[:, 0:128] = rows[:, 128:256]
    first[:, 128:160] = rows[:, 256:288]
    to_halo = nt(hot, outer).astype(BF16)
    to_halo = jnp.concatenate([to_halo, to_halo], axis=1)

    to_left.wait()
    to_right.wait()
    more = first[...] + 0.15 * nn(to_halo, halves(halo[...], 0))
    for r in range(2):
        send[pl.ds(r * 2 + 1, 128, stride=8), :] = more[r * 128:(r + 1) * 128, 0:128]
    lane = iota((128, 128), 1)
    send[pl.ds(4, 128, stride=8), :] = jnp.where(
        lane < 32, more[0:128, 128:256], pltpu.roll(more[128:256, 128:256], 32, axis=1))

    block = lambda ref, d, n: ref.at[pl.ds(pl.multiple_of(d * 8, 8), n)]

    def scatter(d):
        return pltpu.make_async_remote_copy(
            src_ref=block(send, d, 5), dst_ref=block(arr, me, 5), send_sem=send_sem, recv_sem=recv_sem,
            device_id=at(d), device_id_type=MESH)

    @pl.loop(1, ndev)
    def _(k):
        scatter(lax.rem(me + k, ndev)).start()

    mine = pltpu.make_async_copy(block(send, me, 5), block(arr, me, 5), own_sem)
    mine.start()

    mrow, mcol = iota((256, 256), 0), iota((256, 256), 1)
    same = (mrow % 4) == (mcol // 64)
    gap = (mcol % 64 - (((mrow % 8) // 4) * 32 + mrow // 8)) % 64
    move = jnp.where(same & (gap == 0), 1.0, 0.0).astype(BF16)
    mix = jnp.where(same & (gap == 0), 3.0, jnp.where(same & ((gap == 1) | (gap == 63)), 1.0, 0.0)).astype(BF16)

    @pl.loop(0, octs)
    def _(o):
        for copy in loads(o):
            copy.wait()
        for half in range(2):
            quad = o * 2 + half
            lanes = slice(half * 256, half * 256 + 256)
            wt[quad] = nt(mix, ct[o, :, lanes])
            wm[quad] = nt(mix, cm[o, :, lanes])
            ice = nt(move, mk[o, :, lanes].astype(F32).astype(BF16)) > 0.5
            ra[quad] = jnp.where(ice, 0.3, 0.7)
            ga[quad] = jnp.where(ice, 0.39, 0.7)

    tail[0:16, :] = halo[:, 0:128]
    tail[16:128, :] = jnp.zeros((112, 128), F32)
    tmp[0:128, :] = jnp.transpose(tail[...])
    tail[0:16, :] = halo[:, 128:256]
    tmp[128:256, :] = jnp.transpose(tail[...])
    beyond = halves(tmp[16:160, :], 1)
    outer = jnp.concatenate([outer, jnp.zeros((112, 128), BF16)], axis=0)
    near[...] = near[...] + 0.15 * nn(beyond, jnp.concatenate([outer, outer], axis=0))

    everyone = pl.ds(0, (ndev - 1) * 5)
    whole = pltpu.make_async_remote_copy(
        src_ref=send.at[everyone], dst_ref=arr.at[everyone], send_sem=send_sem, recv_sem=recv_sem,
        device_id=at(right), device_id_type=MESH)
    whole.wait_recv()
    mine.wait()

    for part in range(3):
        for r in range(2):
            if part < 2:
                got = arr[pl.ds(r * 2 + part, 128, stride=8), :]
            else:
                got = arr[pl.ds(4, 128, stride=8), :]
                got = pltpu.roll(got, 96, axis=1) if r else got
            tmp[pl.ds(r, 128, stride=2), :] = got
        feat[part * 128:(part + 1) * 128, :] = jnp.transpose(tmp[...])

    upper = iota((8, 128), 0) < 4
    tend[:, 144:256, :] = jnp.zeros((2, 112, 128), F32)

    def giveback(d):
        return pltpu.make_async_remote_copy(
            src_ref=block(rsend, d, 3), dst_ref=block(rarr, me, 3), send_sem=rsend_sem, recv_sem=rrecv_sem,
            device_id=at(d), device_id_type=MESH)

    def peer(h, k):
        return h * 64 + lax.rem(me + k, 64)

    for h in range(2):
        @pl.loop(0, octs)
        def _(o, h=h):
            if h:
                for k in range(7):
                    giveback(peer(0, 1 + o * 7 + k)).start()
            low, high = [], []
            for f in range(4):
                v = feat[pl.ds(pl.multiple_of((f * 9 + o) * 8, 8), 8), h * 128:(h + 1) * 128]
                w = turn(v)
                low.append(jnp.where(upper, v, w))
                high.append(jnp.where(upper, w, v))
            ta, ma = unit(wt, wm, ra, ga, low, o * 2, h)
            tb, mb = unit(wt, wm, ra, ga, high, o * 2 + 1, h)
            tend[h, pl.ds(pl.multiple_of(o * 8, 8), 8), :] = jnp.where(upper, ta, tb)
            tend[h, pl.ds(pl.multiple_of(72 + o * 8, 8), 8), :] = jnp.where(upper, ma, mb)

        tmp[0:128, :] = jnp.transpose(tend[h, 0:128])
        tmp[128:256, :] = jnp.transpose(tend[h, 128:256])
        for r in range(2):
            rsend[pl.ds(h * 512 + r, 64, stride=8), :] = tmp[pl.ds(r, 64, stride=2), :]
        rsend[pl.ds(h * 512 + 2, 64, stride=8), :] = jnp.where(
            iota((64, 128), 1) < 16, tmp[pl.ds(128, 64, stride=2), :],
            pltpu.roll(tmp[pl.ds(129, 64, stride=2), :], 16, axis=1))

    giveback(lax.rem(me + 64, ndev)).start()

    @pl.loop(1, 64)
    def _(k):
        giveback(peer(1, k)).start()

    mine_back = pltpu.make_async_copy(block(rsend, me, 3), block(rarr, me, 3), rown_sem)
    mine_back.start()
    back = pl.ds(0, (ndev - 1) * 3)
    whole_back = pltpu.make_async_remote_copy(
        src_ref=rsend.at[back], dst_ref=rarr.at[back], send_sem=rsend_sem, recv_sem=rrecv_sem,
        device_id=at(right), device_id_type=MESH)
    whole_back.wait_recv()
    mine_back.wait()
    last = jnp.transpose(rarr[pl.ds(2, 128, stride=8), :])
    found = jnp.concatenate([
        jnp.concatenate([jnp.transpose(rarr[pl.ds(r, 128, stride=8), :]), last[r * 16:(r + 1) * 16]], axis=0)
        for r in range(2)], axis=1)
    both = halves(found, 0)
    moved = nn(both, hot)
    out[...] = near[...] + (moved[0:144] + moved[144:288])
    whole.wait_send()
    whole_back.wait_send()


def solution(mesh):
    nsec, nblk = mesh.shape["sec"], mesh.shape["blk"]
    ndev = nsec * nblk
    vmem = pl.BlockSpec(memory_space=pltpu.VMEM)
    hbm = pl.BlockSpec(memory_space=pl.ANY)
    dma = pltpu.SemaphoreType.DMA

    call = pl.pallas_call(
        functools.partial(kernel, nblk, ndev),
        out_shape=jax.ShapeDtypeStruct((144, 128), F32),
        in_specs=[hbm] * 5,
        out_specs=vmem,
        scratch_shapes=[
            pltpu.VMEM((144, 128), F32),
            pltpu.VMEM((4, 128), jnp.int32),
            pltpu.VMEM((1, 128), jnp.int32),
            pltpu.VMEM((9, 256, 512), BF16),
            pltpu.VMEM((9, 256, 512), BF16),
            pltpu.VMEM((9, 256, 512), jnp.int32),
            pltpu.VMEM((18, 256, 256), F32),
            pltpu.VMEM((18, 256, 256), F32),
            pltpu.VMEM((18, 256, 256), F32),
            pltpu.VMEM((18, 256, 256), F32),
            pltpu.VMEM((384, 256), F32),
            pltpu.VMEM((144, 128), F32),
            pltpu.VMEM((256, 128), F32),
            pltpu.VMEM((16, 256), F32),
            pltpu.VMEM((16, 256), F32),
            pltpu.VMEM((1024, 128), F32),
            pltpu.VMEM((1024, 128), F32),
            pltpu.VMEM((256, 256), F32),
            pltpu.VMEM((2, 256, 128), F32),
            pltpu.VMEM((256, 128), F32),
            pltpu.VMEM((128, 128), F32),
            pltpu.VMEM((1024, 128), F32),
            pltpu.VMEM((1024, 128), F32),
            dma((3,)), dma((3, 9)), dma((2,)), dma((2,)), dma, dma, dma, dma, dma, dma,
        ],
        compiler_params=pltpu.CompilerParams(
            collective_id=0, has_side_effects=True, vmem_limit_bytes=56 * 2**20),
        name="gcm_step",
    )

    def local(state, neighbors, owner, crm_state, phase_mask):
        made = call(state.reshape(144, 128), neighbors, owner.reshape(1, 128), crm_state, phase_mask)
        return made.reshape(2, 72, 128)

    both = ("sec", "blk")
    P = jax.sharding.PartitionSpec
    return jax.shard_map(
        local,
        mesh=mesh,
        in_specs=(P(None, None, both), P(None, both), P(both, None), P(both, None), P(both, None)),
        out_specs=P(None, None, both),
        check_vma=False,
    )
```

time: 47.6 us -> 42.4 us (0.89)
  Pallas kernels: 44.5 us -> 40.7 us
  local copies, waits for them, and re-layouts: 2.91 us -> 1.52 us
    pallas_call x1, Pallas kernels: 44.5 us -> 40.7 us  [local(): call(state.reshape(144, 128), neighbors, owner.reshape(1, 128), crm_state...]
    unnamed x2 -> x1, local copies, waits for them, and re-layouts: 2.91 us -> 1.52 us
where the time goes in v2:
time: 42.4 us; the launch traced here: 42.2 us
  Pallas kernels  40.7 us (96%)
  local copies, waits for them, and re-layouts  1.52 us (4%)
    pallas_call x1, Pallas kernels, local(): call(state.reshape(144, 128), neighbors, owner.reshape(1, 128), crm_state...  40.7 us
    unnamed x1, local copies, waits for them, and re-layouts  1.52 us

profile of v2, /device:TPU:7, one launch (start us, length us, event | category | flops | bytes accessed | tf_op | source)
XLA Modules:
  0.0 42.2 jit_solution(229362545250687686)
XLA Ops:
  0.0 40.7 %gcm_step.1 = f32[144,128]{1,0:T(8,128)} custom-call(f32[144,128]{1,0:T(8,128)} %bitcast.4, s32[4,128]{1,0:T(4,128)} %nbr.1, s32[1,128]{1,0:T(1,128)} %bitcast.5, bf16[256,9216]{1,0:T(8,128)(2,1)} %crm.1, s32[256,4608]{1,0:T(8,128)} %mask.1), custom_call_target="tpu_custom_call" | custom-call | tf_op jit(solution)/shard_map/gcm_step/pallas_call | solution.py:360
  40.7 1.5 %copy.7 = f32[2,72,128]{2,1,0:T(8,128)} copy(f32[2,72,128]{2,1,0:T(8,128)} %bitcast.3) | data formatting | bytes 147456

commit v3 on v2

--- a/solution.py
+++ b/solution.py
@@ -1,4 +1,5 @@
 import functools
+import itertools
 import math
 
 import jax
@@ -104,6 +105,10 @@
     return (sum_t * (1.0 / 64) - SHIFT[SUB]) * (1.0 / GROW[SUB]), (sum_m * (1.0 / 64)) * (1.0 / GROW[SUB])
 
 
+def far_first(steps):
+    return sorted(steps, key=lambda t: (-sum(min(d, 4 - d) for d in t[:3]), -t[3]))
+
+
 def kernel(nblk, ndev, state, nbr, own, crm, mask, out,
            st, nb, ow, ct, cm, mk, wt, wm, ra, ga, feat, near, sq, edge, halo, send, arr, first, tend, tmp, tail, rsend, rarr,
            isem, csem, halo_send, halo_recv, send_sem, recv_sem, rsend_sem, rrecv_sem, own_sem, rown_sem):
@@ -111,6 +116,13 @@
     right, left = lax.rem(me + 1, ndev), lax.rem(me + ndev - 1, ndev)
     at = lambda d: (d // nblk, lax.rem(d, nblk))
     octs = 9
+    xat, blk = lax.axis_index("sec"), lax.axis_index("blk")
+    yat, zat, core = blk // 8, lax.rem(blk // 2, 4), lax.rem(blk, 2)
+    xs = [lax.rem(xat + d, 4) for d in range(4)]
+    ys = [lax.rem(yat + d, 4) * 8 for d in range(4)]
+    zs = [lax.rem(zat + d, 4) * 2 for d in range(4)]
+    cs = [core, 1 - core]
+    others = far_first([t for t in itertools.product(range(4), range(4), range(4), range(2)) if any(t)])
 
     small = [pltpu.make_async_copy(state, st, isem.at[0]), pltpu.make_async_copy(nbr, nb, isem.at[1]),
              pltpu.make_async_copy(own, ow, isem.at[2])]
@@ -118,9 +130,8 @@
         copy.start()
     barrier = pltpu.get_barrier_semaphore()
 
-    @pl.loop(1, ndev)
-    def _(k):
-        pl.semaphore_signal(barrier, inc=1, device_id=at(lax.rem(me + k, ndev)), device_id_type=MESH)
+    for dx, dy, dz, dc in others:
+        pl.semaphore_signal(barrier, inc=1, device_id=(xs[dx], ys[dy] + zs[dz] + cs[dc]), device_id_type=MESH)
 
     def loads(o):
         cols = pl.ds(pl.multiple_of(o * 512, 512), 512)
@@ -195,14 +206,13 @@
 
     block = lambda ref, d, n: ref.at[pl.ds(pl.multiple_of(d * 8, 8), n)]
 
-    def scatter(d):
+    def scatter(sec, rest):
         return pltpu.make_async_remote_copy(
-            src_ref=block(send, d, 5), dst_ref=block(arr, me, 5), send_sem=send_sem, recv_sem=recv_sem,
-            device_id=at(d), device_id_type=MESH)
-
-    @pl.loop(1, ndev)
-    def _(k):
-        scatter(lax.rem(me + k, ndev)).start()
+            src_ref=block(send, sec * nblk + rest, 5), dst_ref=block(arr, me, 5), send_sem=send_sem,
+            recv_sem=recv_sem, device_id=(sec, rest), device_id_type=MESH)
+
+    for dx, dy, dz, dc in others:
+        scatter(xs[dx], ys[dy] + zs[dz] + cs[dc]).start()
 
     mine = pltpu.make_async_copy(block(send, me, 5), block(arr, me, 5), own_sem)
     mine.start()
@@ -255,20 +265,18 @@
     upper = iota((8, 128), 0) < 4
     tend[:, 144:256, :] = jnp.zeros((2, 112, 128), F32)
 
-    def giveback(d):
+    def giveback(sec, rest):
         return pltpu.make_async_remote_copy(
-            src_ref=block(rsend, d, 3), dst_ref=block(rarr, me, 3), send_sem=rsend_sem, recv_sem=rrecv_sem,
-            device_id=at(d), device_id_type=MESH)
-
-    def peer(h, k):
-        return h * 64 + lax.rem(me + k, 64)
+            src_ref=block(rsend, sec * nblk + rest, 3), dst_ref=block(rarr, me, 3), send_sem=rsend_sem,
+            recv_sem=rrecv_sem, device_id=(sec, rest), device_id_type=MESH)
 
     for h in range(2):
         @pl.loop(0, octs)
         def _(o, h=h):
             if h:
                 for k in range(7):
-                    giveback(peer(0, 1 + o * 7 + k)).start()
+                    d = lax.rem(me + 1 + o * 7 + k, 64)
+                    giveback(d // nblk, lax.rem(d, nblk)).start()
             low, high = [], []
             for f in range(4):
                 v = feat[pl.ds(pl.multiple_of((f * 9 + o) * 8, 8), 8), h * 128:(h + 1) * 128]
@@ -288,11 +296,10 @@
             iota((64, 128), 1) < 16, tmp[pl.ds(128, 64, stride=2), :],
             pltpu.roll(tmp[pl.ds(129, 64, stride=2), :], 16, axis=1))
 
-    giveback(lax.rem(me + 64, ndev)).start()
-
-    @pl.loop(1, 64)
-    def _(k):
-        giveback(peer(1, k)).start()
+    sides = [2 + lax.rem(xat, 2), 2 + lax.rem(xat + 1, 2)]
+    for dx, dy, dz, dc in far_first([t for t in itertools.product(range(2), range(4), range(4), range(2)) if any(t)]):
+        giveback(sides[dx], ys[dy] + zs[dz] + cs[dc]).start()
+    giveback(xs[2], blk).start()
 
     mine_back = pltpu.make_async_copy(block(rsend, me, 3), block(rarr, me, 3), rown_sem)
     mine_back.start()
@@ -317,7 +324,7 @@
     nsec, nblk = mesh.shape["sec"], mesh.shape["blk"]
     ndev = nsec * nblk
     vmem = pl.BlockSpec(memory_space=pltpu.VMEM)
-    hbm = pl.BlockSpec(memory_space=pl.ANY)
+    hbm = pl.BlockSpec(memory_space=pltpu.HBM)
     dma = pltpu.SemaphoreType.DMA
 
     call = pl.pallas_call(
@@ -352,12 +359,13 @@
             dma((3,)), dma((3, 9)), dma((2,)), dma((2,)), dma, dma, dma, dma, dma, dma,
         ],
         compiler_params=pltpu.CompilerParams(
-            collective_id=0, has_side_effects=True, vmem_limit_bytes=56 * 2**20),
+            collective_id=0, has_side_effects=True, vmem_limit_bytes=44 * 2**20),
         name="gcm_step",
     )
 
     def local(state, neighbors, owner, crm_state, phase_mask):
-        made = call(state.reshape(144, 128), neighbors, owner.reshape(1, 128), crm_state, phase_mask)
+        keep = lambda a: pltpu.with_memory_space_constraint(a, pltpu.HBM)
+        made = call(keep(state.reshape(144, 128)), keep(neighbors), keep(owner.reshape(1, 128)), keep(crm_state), keep(phase_mask))
         return made.reshape(2, 72, 128)
 
     both = ("sec", "blk")

time: 42.4 us -> 37.7 us (0.89)
  the two profiles are of different devices: /device:TPU:7 before, /device:TPU:1 now
where the time goes in v3:
time: 37.7 us; the launch traced here: 37.6 us
  Pallas kernels  36.9 us (98%)
  local copies, waits for them, and re-layouts  0.64 us (2%)
    pallas_call x1, Pallas kernels, local(): call(keep(state.reshape(144, 128)), keep(neighbors), keep(owner.reshape(1...  36.9 us

profile of v3, /device:TPU:1, one launch (start us, length us, event | category | flops | bytes accessed | tf_op | source)
XLA Modules:
  0.0 37.6 jit_solution(8305121543709256100)
XLA Ops:
  0.0 36.9 %gcm_step.1 = f32[144,128]{1,0:T(8,128)S(1)} custom-call(f32[144,128]{1,0:T(8,128)} %bitcast.4, s32[4,128]{1,0:T(4,128)} %nbr.1, s32[1,128]{1,0:T(1,128)} %bitcast.5, bf16[256,9216]{1,0:T(8,128)(2,1)} %crm.1, s32[256,4608]{1,0:T(8,128)} %mask.1), custom_call_target="tpu_custom_call" | custom-call | tf_op jit(solution)/shard_map/gcm_step/pallas_call | solution.py:368
  36.9 0.6 %copy.7 = f32[2,72,128]{2,1,0:T(8,128)} copy(f32[2,72,128]{2,1,0:T(8,128)S(1)} %bitcast.3) | data formatting | bytes 147456

commit v4 on v3

v4 whole, which is shorter than its diff:
```python
import functools
import itertools
import math

import jax
import jax.numpy as jnp
from jax import lax
from jax.experimental import pallas as pl
from jax.experimental.pallas import tpu as pltpu

SUB = 4
REACH = 8
F32 = jnp.float32
BF16 = jnp.bfloat16
MESH = pl.DeviceIdType.MESH

GROW = [5.0 ** k for k in range(SUB + 1)]
SHIFT = [GROW[k] * (math.log(0.8) + k * math.log(5.0)) / 0.3 for k in range(SUB + 1)]
UNIT = 0.3 * math.log2(math.e) / GROW[1]


def nt(a, b):
    return lax.dot_general(a, b, (((1,), (1,)), ((), ())), preferred_element_type=F32)


def nn(a, b):
    return lax.dot_general(a, b, (((1,), (0,)), ((), ())), preferred_element_type=F32)


def halves(a, dim):
    high = a.astype(BF16)
    return jnp.concatenate([high, (a - high.astype(F32)).astype(BF16)], axis=dim)


def iota(shape, dim):
    return lax.broadcasted_iota(jnp.int32, shape, dim)


def turn(v):
    return pltpu.roll(v, 4, axis=0)


def unit(wt, wm, ra, ga, column, quad, h):
    tcol, mcol, tforce, mforce = column
    tadd = [None] + [tforce * (UNIT * GROW[k] / SUB) + UNIT * (SHIFT[k] - (5.0 * SHIFT[k - 1] if k > 1 else 0.0)) for k in range(1, SUB + 1)]
    madd = [None] + [mforce * (GROW[k] / SUB) for k in range(1, SUB + 1)]
    tadd[1] = tadd[1] + (5.0 * UNIT) * tcol
    madd[1] = madd[1] + 5.0 * mcol
    rate, gain = {}, {}

    def coeffs(j):
        if j not in rate:
            rows = slice((j % 32) * 8, (j % 32) * 8 + 8)
            rate[j], gain[j] = ra[h, quad, rows, :], ga[h, quad, rows, :]
            if j >= 32:
                rate[j], gain[j] = turn(rate[j]), turn(gain[j])
        return rate[j], gain[j]

    temps = [{} for _ in range(SUB + 1)]
    moists = [{} for _ in range(SUB + 1)]
    tpair = [{} for _ in range(SUB + 1)]
    mpair = [{} for _ in range(SUB + 1)]
    sums = [[] for _ in range(4)]
    rates, poss = {}, {}

    def condense(k, j, t, m):
        r, g = coeffs(j)
        pos = jnp.maximum(m - jnp.exp2(t * (GROW[1] / GROW[k]) if k > 1 else t), 0.0)
        if k == SUB:
            temps[k][j], moists[k][j], rates[j], poss[j] = t, m, r * pos, pos
            return
        temps[k][j] = t + g * pos
        moists[k][j] = m - r * pos

    def get(store, k, j):
        if j not in store[k]:
            store[k][j] = turn(store[k][j - 32])
        return store[k][j]

    def pair(store, pairs, k, j):
        if j not in pairs[k]:
            pairs[k][j] = get(store, k, j - 1) + get(store, k, j)
        return pairs[k][j]

    def spread(store, pairs, k, j):
        return (pair(store, pairs, k, j) + get(store, k, j)) + pair(store, pairs, k, j + 1)

    for step in range(32 + 2 * SUB):
        if step < 32:
            rows = slice(step * 8, step * 8 + 8)
            condense(1, step, wt[h, quad, rows, :] + tadd[1], wm[h, quad, rows, :] + madd[1])
        for k in range(2, SUB + 1):
            j = step - (k - 1)
            if k - 1 <= j < k - 1 + 32:
                t = spread(temps, tpair, k - 1, j) + tadd[k]
                m = spread(moists, mpair, k - 1, j) + madd[k]
                condense(k, j, t, m)
                if k == SUB:
                    for s, v in zip(sums, (t, m, rates[j], poss[j])):
                        s.append(v)
                        if len(s) > 2:
                            s[:] = [s[1], s[0] + s[2]]
    sum_t, sum_m, sum_c, sum_p = [s[0] + s[1] for s in sums]
    sum_t = sum_t + UNIT * (0.1575 * sum_p + 0.775 * sum_c)
    sum_m = sum_m - sum_c
    sum_t = sum_t + turn(sum_t)
    sum_m = sum_m + turn(sum_m)
    return (sum_t * (1.0 / (64 * UNIT)) - SHIFT[SUB]) * (1.0 / GROW[SUB]), (sum_m * (1.0 / 64)) * (1.0 / GROW[SUB])


def far_first(steps):
    return sorted(steps, key=lambda t: (-sum(min(d, 4 - d) for d in t[:3]), -t[3]))


def kernel(nblk, ndev, state, nbr, own, crm, mask, out,
           st, nb, ow, ct, cm, mk, wt, wm, ra, ga, hots, feat_far, feat_near, near, sq, edge, halo, send, arr, first, tend_far, tend_near, tmp, tmp_near, back, rsend, rarr,
           isem, csem, halo_send, halo_recv, send_sem, recv_sem, rsend_sem, rrecv_sem, own_sem, rown_sem, lines_sem, planes_sem):
    me = lax.axis_index("sec") * nblk + lax.axis_index("blk")
    right, left = lax.rem(me + 1, ndev), lax.rem(me + ndev - 1, ndev)
    at = lambda d: (d // nblk, lax.rem(d, nblk))
    octs = 9
    xat, blk = lax.axis_index("sec"), lax.axis_index("blk")
    yat, zat, core = blk // 8, lax.rem(blk // 2, 4), lax.rem(blk, 2)
    xs = [lax.rem(xat + d, 4) for d in range(4)]
    ys = [lax.rem(yat + d, 4) * 8 for d in range(4)]
    zs = [lax.rem(zat + d, 4) * 2 for d in range(4)]
    cs = [core, 1 - core]
    others = far_first([t for t in itertools.product(range(4), range(4), range(4), range(2)) if any(t)])

    small = [pltpu.make_async_copy(state, st, isem.at[0]), pltpu.make_async_copy(nbr, nb, isem.at[1]),
             pltpu.make_async_copy(own, ow, isem.at[2])]
    for copy in small:
        copy.start()
    barrier = pltpu.get_barrier_semaphore()

    def tell(sem, steps):
        for dx, dy, dz, dc in far_first(steps):
            pl.semaphore_signal(sem, inc=1, device_id=(xs[dx], ys[dy] + zs[dz] + cs[dc]), device_id_type=MESH)

    along_x = [(d, 0, 0, 0) for d in range(1, 4)]
    along_y = [(0, d, 0, 0) for d in range(1, 4)]
    group_z = [(0, 0, d, c) for d in range(4) for c in range(2) if d or c]
    for d in (left, right):
        pl.semaphore_signal(barrier, inc=1, device_id=at(d), device_id_type=MESH)
    tell(barrier, along_x + along_y + group_z)

    def loads(o):
        cols = pl.ds(pl.multiple_of(o * 512, 512), 512)
        mcols = pl.ds(pl.multiple_of(4608 + o * 512, 512), 512)
        return [
            pltpu.make_async_copy(crm.at[:, cols], ct.at[o], csem.at[0, o]),
            pltpu.make_async_copy(crm.at[:, mcols], cm.at[o], csem.at[1, o]),
            pltpu.make_async_copy(mask.at[:, cols], mk.at[o], csem.at[2, o]),
        ]

    for copy in small:
        copy.wait()

    @pl.loop(0, octs)
    def _(o):
        for copy in loads(o):
            copy.start()

    sq[0:16, :] = jnp.zeros((16, 128), F32)
    sq[16:160, :] = st[...]
    sq[160:256, :] = jnp.zeros((96, 128), F32)
    pick_row, pick_col = iota((16, 128), 0), iota((16, 128), 1)
    pick = jnp.where(pick_col == jnp.where(pick_row < 8, pick_row, pick_row + 112), 1.0, 0.0).astype(BF16)
    edge[...] = nt(jnp.concatenate([pick, pick], axis=1), halves(sq[...], 1))

    pl.semaphore_wait(barrier, 15)
    to_left = pltpu.make_async_remote_copy(
        src_ref=edge.at[0:8], dst_ref=halo.at[8:16], send_sem=halo_send.at[0], recv_sem=halo_recv.at[0],
        device_id=at(left), device_id_type=MESH)
    to_right = pltpu.make_async_remote_copy(
        src_ref=edge.at[8:16], dst_ref=halo.at[0:8], send_sem=halo_send.at[1], recv_sem=halo_recv.at[1],
        device_id=at(right), device_id_type=MESH)
    to_left.start()
    to_right.start()
    tell(lines_sem, along_y)

    pl.semaphore_wait(lines_sem, 3)
    tell(planes_sem, group_z)

    row, col = iota((128, 128), 0), iota((128, 128), 1)
    own_across = ow[...]
    own_down = jnp.sum(jnp.where(row == col, own_across, 0), axis=1, keepdims=True)
    rank = jnp.sum(jnp.where((own_down == own_across) & (row < col), 1, 0), axis=0, keepdims=True)
    hot = jnp.concatenate(
        [jnp.where((row == own_across) & (rank == r), 1.0, 0.0).astype(BF16) for r in range(2)], axis=0)
    place = nb[...] - (me * 128 - REACH)
    place = jnp.where(place < 0, place + ndev * 128, place)
    place = jnp.where(place >= ndev * 128, place - ndev * 128, place)
    inner = jnp.where(row == col, -4.0, 0.0)
    halo_row = iota((16, 128), 0)
    halo_place = jnp.where(halo_row < 8, halo_row, halo_row + 128)
    outer = jnp.zeros((16, 128), F32)
    for k in range(4):
        p = place[k:k + 1, :]
        inner = inner + jnp.where(p == row + REACH, 1.0, 0.0)
        outer = outer + jnp.where(p == halo_place, 1.0, 0.0)
    inner, outer = inner.astype(BF16), outer.astype(BF16)
    near[...] = 0.15 * nn(halves(st[...], 1), jnp.concatenate([inner, inner], axis=0))
    hots[...] = hot
    hot_twice = jnp.concatenate([hot, hot], axis=1)
    rows = nt(hot_twice, jnp.concatenate([halves(st[...], 1), halves(near[...], 1)], axis=0))
    for r in range(2):
        send[pl.ds(r * 2, 128, stride=8), :] = rows[r * 128:(r + 1) * 128, 0:128]
    first[:, 0:128] = rows[:, 128:256]
    first[:, 128:160] = rows[:, 256:288]
    to_halo = nt(hot, outer).astype(BF16)
    to_halo = jnp.concatenate([to_halo, to_halo], axis=1)

    to_left.wait()
    to_right.wait()
    pl.semaphore_wait(planes_sem, 7)
    more = first[...] + 0.15 * nn(to_halo, halves(halo[...], 0))
    for r in range(2):
        send[pl.ds(r * 2 + 1, 128, stride=8), :] = more[r * 128:(r + 1) * 128, 0:128]
    lane = iota((128, 128), 1)
    send[pl.ds(4, 128, stride=8), :] = jnp.where(
        lane < 32, more[0:128, 128:256], pltpu.roll(more[128:256, 128:256], 32, axis=1))

    block = lambda ref, d, n: ref.at[pl.ds(pl.multiple_of(d * 8, 8), n)]

    def scatter(sec, rest, group):
        return pltpu.make_async_remote_copy(
            src_ref=block(send, sec * nblk + rest, 5), dst_ref=block(arr, me, 5), send_sem=send_sem,
            recv_sem=recv_sem.at[group], device_id=(sec, rest), device_id_type=MESH)

    group = [1 - lax.rem(x // 2 + xat // 2, 2) for x in xs]
    for dx, dy, dz, dc in others:
        scatter(xs[dx], ys[dy] + zs[dz] + cs[dc], group[dx]).start()

    mine = pltpu.make_async_copy(block(send, me, 5), block(arr, me, 5), own_sem)
    mine.start()

    mrow, mcol = iota((256, 256), 0), iota((256, 256), 1)
    same = (mrow % 4) == (mcol // 64)
    gap = (mcol % 64 - (((mrow % 8) // 4) * 32 + mrow // 8)) % 64
    move = jnp.where(same & (gap == 0), 1.0, 0.0).astype(BF16)
    mix = jnp.where(same & (gap == 0), 3.0, jnp.where(same & ((gap == 1) | (gap == 63)), 1.0, 0.0)).astype(BF16)

    @pl.loop(0, octs)
    def _(o):
        for copy in loads(o):
            copy.wait()
        for half in range(2):
            quad = o * 2 + half
            lanes = slice(half * 256, half * 256 + 256)
            ice = nt(move, mk[o, :, lanes].astype(F32).astype(BF16)) > 0.5
            made = (UNIT * nt(mix, ct[o, :, lanes]), nt(mix, cm[o, :, lanes]),
                    jnp.where(ice, 0.3, 0.7), jnp.where(ice, 0.39 * UNIT, 0.7 * UNIT))
            for h in range(2):
                for ref, value in zip((wt, wm, ra, ga), made):
                    ref[h, quad] = value[:, h * 128:(h + 1) * 128]

    for part in range(2):
        tmp[part, 0:16, :] = halo[:, part * 128:(part + 1) * 128]
        tmp[part, 16:128, :] = jnp.zeros((112, 128), F32)
    beyond = jnp.concatenate([jnp.transpose(tmp[0])[16:128], jnp.transpose(tmp[1])[0:32]], axis=0)
    beyond = halves(beyond, 1)
    outer = jnp.concatenate([outer, jnp.zeros((112, 128), BF16)], axis=0)
    near[...] = near[...] + 0.15 * nn(beyond, jnp.concatenate([outer, outer], axis=0))

    def all_sent(copies, group):
        rows = pl.ds(0, copies * 5)
        return pltpu.make_async_remote_copy(
            src_ref=send.at[rows], dst_ref=arr.at[rows], send_sem=send_sem, recv_sem=recv_sem.at[group],
            device_id=at(right), device_id_type=MESH)

    def arrive(h, feat, tmp):
        for part in range(3):
            for r in range(2):
                start = h * 512 + (4 if part == 2 else r * 2 + part)
                got = arr[pl.ds(start, 64, stride=8), :]
                if part == 2 and r:
                    got = pltpu.roll(got, 96, axis=1)
                tmp[part, pl.ds(r, 64, stride=2), :] = got
            feat[part * 128:(part + 1) * 128, :] = jnp.transpose(tmp[part])

    upper = iota((8, 128), 0) < 4
    for tend in (tend_far, tend_near):
        tend[144:256, :] = jnp.zeros((112, 128), F32)

    def giveback(sec, rest, group):
        return pltpu.make_async_remote_copy(
            src_ref=block(rsend, sec * nblk + rest, 3), dst_ref=block(rarr, me, 3), send_sem=rsend_sem,
            recv_sem=rrecv_sem.at[group], device_id=(sec, rest), device_id_type=MESH)

    def octet(o, h, feat, tend):
        low, high = [], []
        for f in range(4):
            v = feat[pl.ds(pl.multiple_of((f * 9 + o) * 8, 8), 8), :]
            w = turn(v)
            low.append(jnp.where(upper, v, w))
            high.append(jnp.where(upper, w, v))
        ta, ma = unit(wt, wm, ra, ga, low, o * 2, h)
        tb, mb = unit(wt, wm, ra, ga, high, o * 2 + 1, h)
        tend[pl.ds(pl.multiple_of(o * 8, 8), 8), :] = jnp.where(upper, ta, tb)
        tend[pl.ds(pl.multiple_of(72 + o * 8, 8), 8), :] = jnp.where(upper, ma, mb)

    def pack(h, tend):
        for part in range(2):
            back[part] = jnp.transpose(tend[part * 128:(part + 1) * 128])
        for r in range(2):
            rsend[pl.ds(h * 512 + r, 64, stride=8), :] = back[0, pl.ds(r, 64, stride=2), :]
        rsend[pl.ds(h * 512 + 2, 64, stride=8), :] = jnp.where(
            iota((64, 128), 1) < 16, back[1, pl.ds(0, 64, stride=2), :],
            pltpu.roll(back[1, pl.ds(1, 64, stride=2), :], 16, axis=1))

    near_half = xat // 2
    far_half = 1 - near_half
    all_sent(ndev // 2 - 1, 1).wait_recv()
    mine.wait()
    arrive(near_half, feat_near, tmp_near)
    all_sent(ndev // 2, 0).wait_recv()
    arrive(far_half, feat_far, tmp)
    octet(0, far_half, feat_far, tend_far)

    @pl.loop(1, octs)
    def _(o):
        octet(o, far_half, feat_far, tend_far)

    pack(far_half, tend_far)
    octet(0, near_half, feat_near, tend_near)

    @pl.loop(1, octs)
    def _(o):
        for k in range(8):
            giveback(far_half * 2 + k % 2, (o - 1) * 4 + k // 2, 0).start()
        octet(o, near_half, feat_near, tend_near)

    pack(near_half, tend_near)
    sides = [xat, near_half * 2 + 1 - lax.rem(xat, 2)]
    for dx, dy, dz, dc in far_first([t for t in itertools.product(range(2), range(4), range(4), range(2)) if any(t)]):
        giveback(sides[dx], ys[dy] + zs[dz] + cs[dc], 1).start()

    mine_back = pltpu.make_async_copy(block(rsend, me, 3), block(rarr, me, 3), rown_sem)
    mine_back.start()

    def all_of(copies, group):
        rows = pl.ds(0, copies * 3)
        return pltpu.make_async_remote_copy(
            src_ref=rsend.at[rows], dst_ref=rarr.at[rows], send_sem=rsend_sem, recv_sem=rrecv_sem.at[group],
            device_id=at(right), device_id_type=MESH)

    def settle(half):
        ranks = [rarr[pl.ds(half * 512 + r, 64, stride=8), :] for r in range(2)]
        rest = rarr[pl.ds(half * 512 + 2, 64, stride=8), :]
        found = jnp.concatenate([
            jnp.transpose(jnp.concatenate(ranks, axis=0)),
            jnp.transpose(jnp.concatenate([rest, pltpu.roll(rest, 112, axis=1)], axis=0))[0:16]], axis=0)
        take = jnp.concatenate(
            [hots[pl.ds(pl.multiple_of(r * 128 + half * 64, 64), 64), :] for r in range(2)], axis=0)
        moved = nn(halves(found, 0), take)
        return moved[0:144] + moved[144:288]

    all_of(ndev // 2, 0).wait_recv()
    near[...] = near[...] + settle(far_half)
    all_of(ndev // 2 - 1, 1).wait_recv()
    mine_back.wait()
    out[...] = near[...] + settle(near_half)
    all_sent(ndev - 1, 0).wait_send()
    all_of(ndev - 1, 0).wait_send()


def solution(mesh):
    nsec, nblk = mesh.shape["sec"], mesh.shape["blk"]
    ndev = nsec * nblk
    vmem = pl.BlockSpec(memory_space=pltpu.VMEM)
    hbm = pl.BlockSpec(memory_space=pltpu.HBM)
    dma = pltpu.SemaphoreType.DMA

    call = pl.pallas_call(
        functools.partial(kernel, nblk, ndev),
        out_shape=jax.ShapeDtypeStruct((144, 128), F32),
        in_specs=[hbm] * 5,
        out_specs=vmem,
        scratch_shapes=[
            pltpu.VMEM((144, 128), F32),
            pltpu.VMEM((4, 128), jnp.int32),
            pltpu.VMEM((1, 128), jnp.int32),
            pltpu.VMEM((9, 256, 512), BF16),
            pltpu.VMEM((9, 256, 512), BF16),
            pltpu.VMEM((9, 256, 512), jnp.int32),
            pltpu.VMEM((2, 18, 256, 128), F32),
            pltpu.VMEM((2, 18, 256, 128), F32),
            pltpu.VMEM((2, 18, 256, 128), F32),
            pltpu.VMEM((2, 18, 256, 128), F32),
            pltpu.VMEM((256, 128), BF16),
            pltpu.VMEM((384, 128), F32),
            pltpu.VMEM((384, 128), F32),
            pltpu.VMEM((144, 128), F32),
            pltpu.VMEM((256, 128), F32),
            pltpu.VMEM((16, 256), F32),
            pltpu.VMEM((16, 256), F32),
            pltpu.VMEM((1024, 128), F32),
            pltpu.VMEM((1024, 128), F32),
            pltpu.VMEM((256, 256), F32),
            pltpu.VMEM((256, 128), F32),
            pltpu.VMEM((256, 128), F32),
            pltpu.VMEM((3, 128, 128), F32),
            pltpu.VMEM((3, 128, 128), F32),
            pltpu.VMEM((2, 128, 128), F32),
            pltpu.VMEM((1024, 128), F32),
            pltpu.VMEM((1024, 128), F32),
            dma((3,)), dma((3, 9)), dma((2,)), dma((2,)), dma, dma((2,)), dma, dma((2,)), dma, dma,
            pltpu.SemaphoreType.REGULAR, pltpu.SemaphoreType.REGULAR,
        ],
        compiler_params=pltpu.CompilerParams(
            collective_id=0, has_side_effects=True, vmem_limit_bytes=44 * 2**20),
        name="gcm_step",
    )

    def local(state, neighbors, owner, crm_state, phase_mask):
        keep = lambda a: pltpu.with_memory_space_constraint(a, pltpu.HBM)
        made = call(keep(state.reshape(144, 128)), keep(neighbors), keep(owner.reshape(1, 128)), keep(crm_state), keep(phase_mask))
        return made.reshape(2, 72, 128)

    both = ("sec", "blk")
    P = jax.sharding.PartitionSpec
    return jax.shard_map(
        local,
        mesh=mesh,
        in_specs=(P(None, None, both), P(None, both), P(both, None), P(both, None), P(both, None)),
        out_specs=P(None, None, both),
        check_vma=False,
    )
```

time: 37.7 us -> 36.3 us (0.963)
  Pallas kernels: 36.9 us -> 35.5 us
    pallas_call x1, Pallas kernels: 36.9 us -> 35.5 us  [local(): call(keep(state.reshape(144, 128)), keep(neighbors), keep(owner.reshape(1...]
where the time goes in v4:
time: 36.3 us; the launch traced here: 36.2 us
  Pallas kernels  35.5 us (98%)
  local copies, waits for them, and re-layouts  0.64 us (2%)
    pallas_call x1, Pallas kernels, local(): call(keep(state.reshape(144, 128)), keep(neighbors), keep(owner.reshape(1...  35.5 us

profile of v4, /device:TPU:1, one launch (start us, length us, event | category | flops | bytes accessed | tf_op | source)
XLA Modules:
  0.0 36.2 jit_solution(1115849370197398134)
XLA Ops:
  0.0 35.5 %gcm_step.1 = f32[144,128]{1,0:T(8,128)S(1)} custom-call(f32[144,128]{1,0:T(8,128)} %bitcast.4, s32[4,128]{1,0:T(4,128)} %nbr.1, s32[1,128]{1,0:T(1,128)} %bitcast.5, bf16[256,9216]{1,0:T(8,128)(2,1)} %crm.1, s32[256,4608]{1,0:T(8,128)} %mask.1), custom_call_target="tpu_custom_call" | custom-call | tf_op jit(solution)/shard_map/gcm_step/pallas_call | solution.py:418
  35.5 0.6 %copy.7 = f32[2,72,128]{2,1,0:T(8,128)} copy(f32[2,72,128]{2,1,0:T(8,128)S(1)} %bitcast.3) | data formatting | bytes 147456

commit v5 on v4

--- a/solution.py
+++ b/solution.py
@@ -114,7 +114,7 @@
 
 def kernel(nblk, ndev, state, nbr, own, crm, mask, out,
            st, nb, ow, ct, cm, mk, wt, wm, ra, ga, hots, feat_far, feat_near, near, sq, edge, halo, send, arr, first, tend_far, tend_near, tmp, tmp_near, back, rsend, rarr,
-           isem, csem, halo_send, halo_recv, send_sem, recv_sem, rsend_sem, rrecv_sem, own_sem, rown_sem, lines_sem, planes_sem):
+           isem, csem, halo_send, halo_recv, send_sem, recv_sem, rsend_sem, rrecv_sem, own_sem, rown_sem, planes_sem):
     me = lax.axis_index("sec") * nblk + lax.axis_index("blk")
     right, left = lax.rem(me + 1, ndev), lax.rem(me + ndev - 1, ndev)
     at = lambda d: (d // nblk, lax.rem(d, nblk))
@@ -129,20 +129,19 @@
 
     small = [pltpu.make_async_copy(state, st, isem.at[0]), pltpu.make_async_copy(nbr, nb, isem.at[1]),
              pltpu.make_async_copy(own, ow, isem.at[2])]
-    for copy in small:
-        copy.start()
     barrier = pltpu.get_barrier_semaphore()
 
     def tell(sem, steps):
         for dx, dy, dz, dc in far_first(steps):
             pl.semaphore_signal(sem, inc=1, device_id=(xs[dx], ys[dy] + zs[dz] + cs[dc]), device_id_type=MESH)
 
-    along_x = [(d, 0, 0, 0) for d in range(1, 4)]
-    along_y = [(0, d, 0, 0) for d in range(1, 4)]
+    plane = [(d, e, 0, 0) for d in range(4) for e in range(4) if d or e]
     group_z = [(0, 0, d, c) for d in range(4) for c in range(2) if d or c]
     for d in (left, right):
         pl.semaphore_signal(barrier, inc=1, device_id=at(d), device_id_type=MESH)
-    tell(barrier, along_x + along_y + group_z)
+    tell(barrier, plane + group_z)
+    for copy in small:
+        copy.start()
 
     def loads(o):
         cols = pl.ds(pl.multiple_of(o * 512, 512), 512)
@@ -168,7 +167,7 @@
     pick = jnp.where(pick_col == jnp.where(pick_row < 8, pick_row, pick_row + 112), 1.0, 0.0).astype(BF16)
     edge[...] = nt(jnp.concatenate([pick, pick], axis=1), halves(sq[...], 1))
 
-    pl.semaphore_wait(barrier, 15)
+    pl.semaphore_wait(barrier, 24)
     to_left = pltpu.make_async_remote_copy(
         src_ref=edge.at[0:8], dst_ref=halo.at[8:16], send_sem=halo_send.at[0], recv_sem=halo_recv.at[0],
         device_id=at(left), device_id_type=MESH)
@@ -177,9 +176,6 @@
         device_id=at(right), device_id_type=MESH)
     to_left.start()
     to_right.start()
-    tell(lines_sem, along_y)
-
-    pl.semaphore_wait(lines_sem, 3)
     tell(planes_sem, group_z)
 
     row, col = iota((128, 128), 0), iota((128, 128), 1)
@@ -406,7 +402,7 @@
             pltpu.VMEM((1024, 128), F32),
             pltpu.VMEM((1024, 128), F32),
             dma((3,)), dma((3, 9)), dma((2,)), dma((2,)), dma, dma((2,)), dma, dma((2,)), dma, dma,
-            pltpu.SemaphoreType.REGULAR, pltpu.SemaphoreType.REGULAR,
+            pltpu.SemaphoreType.REGULAR,
         ],
         compiler_params=pltpu.CompilerParams(
             collective_id=0, has_side_effects=True, vmem_limit_bytes=44 * 2**20),

time: 36.3 us -> 36.1 us (level)
  no operation moved by 1% of the time
where the time goes in v5:
time: 36.1 us; the launch traced here: 35.9 us
  Pallas kernels  35.3 us (98%)
  local copies, waits for them, and re-layouts  0.64 us (2%)
    pallas_call x1, Pallas kernels, local(): call(keep(state.reshape(144, 128)), keep(neighbors), keep(owner.reshape(1...  35.3 us

profile of v5, /device:TPU:1, one launch (start us, length us, event | category | flops | bytes accessed | tf_op | source)
XLA Modules:
  0.0 35.9 jit_solution(6378925279299961644)
XLA Ops:
  0.0 35.3 %gcm_step.1 = f32[144,128]{1,0:T(8,128)S(1)} custom-call(f32[144,128]{1,0:T(8,128)} %bitcast.4, s32[4,128]{1,0:T(4,128)} %nbr.1, s32[1,128]{1,0:T(1,128)} %bitcast.5, bf16[256,9216]{1,0:T(8,128)(2,1)} %crm.1, s32[256,4608]{1,0:T(8,128)} %mask.1), custom_call_target="tpu_custom_call" | custom-call | tf_op jit(solution)/shard_map/gcm_step/pallas_call | solution.py:414
  35.3 0.6 %copy.7 = f32[2,72,128]{2,1,0:T(8,128)} copy(f32[2,72,128]{2,1,0:T(8,128)S(1)} %bitcast.3) | data formatting | bytes 147456
